TPU v7x, 32 devices: a whole 2x2x4 slice. The times are simulated.
32 devices in a mesh: sp: 16 (over z, y, core), flt: 2 (over x).
Axes of the slice: x: 2, y: 2, z: 4, core: 2. Of those that a mesh axis runs over, the one named last changes fastest.
Arguments:
- activations: bfloat16 [32, 16, 8, 256], P('sp', 'flt'), may hold values from -6 to 6
- w_first: bfloat16 [256, 3, 3, 3, 256], P('flt'), may hold values from -0.078125 to 0.078125
- w_second: bfloat16 [256, 3, 3, 3, 256], P('flt'), may hold values from -0.078125 to 0.078125
- cotangent: bfloat16 [16, 8, 4, 256], P('sp', 'flt'), may hold values from -6 to 6
Outputs:
- section_out: float32 [16, 8, 4, 256], P('sp', 'flt')
- grad_input: float32 [32, 16, 8, 256], P('sp', 'flt')
- grad_first: float32 [256, 3, 3, 3, 256], P('flt')
- grad_second: float32 [256, 3, 3, 3, 256], P('flt')
All inputs are finite; a program needn't handle non-finite values.
Results may differ from a plain program's by a relative error of at most 0.0045.
Values may be sent and summed in bfloat16 or wider, within the bound.
A program may use at most 64 MiB of HBM per device.

v0:
```python
import functools

import jax
import jax.numpy as jnp
from jax import lax
from jax.experimental import pallas as pl
from jax.experimental.pallas import tpu as pltpu
from jax.sharding import PartitionSpec as P

MESH = pl.DeviceIdType.MESH
VMEM = pl.BlockSpec(memory_space=pltpu.VMEM)
ROOM = 62 * 1024 * 1024


def remote(src, dst, send, recv, place):
    return pltpu.make_async_remote_copy(
        src_ref=src, dst_ref=dst, send_sem=send, recv_sem=recv, device_id=place, device_id_type=MESH
    )


def greet(places):
    barrier = pltpu.get_barrier_semaphore()
    for place in places:
        pl.semaphore_signal(barrier, inc=1, device_id=place, device_id_type=MESH)
    pl.semaphore_wait(barrier, len(places))


def line_kernel(count, own, out, local, recv, send_z, send_y, send_c):
    here, other = lax.axis_index("sp"), lax.axis_index("flt")
    deep = count // 4
    z, y, core = here // 4, (here // 2) % 2, here % 2

    def spot(zz, yy, cc):
        return (zz * 2 + yy) * 2 + cc

    far = [lax.rem(z + step, deep) for step in range(1, deep)]
    to_y = (spot(z, 1 - y, core), other)
    to_c = (spot(z, y, 1 - core), other)
    greet([(spot(zz, y, core), other) for zz in far] + [to_y, to_c])
    sends = []

    def push(src, slot, send, place):
        copy = remote(src, out.at[slot], send, recv.at[slot], place)
        copy.start()
        sends.append(copy)

    def arrived(slot):
        remote(own, out.at[slot], send_y.at[0], recv.at[slot], to_y).wait_recv()

    for n, zz in enumerate(far):
        push(own, here, send_z.at[n], (spot(zz, y, core), other))
    push(own, here, send_y.at[0], to_y)
    push(own, here, send_c.at[0], to_c)
    keep = pltpu.make_async_copy(own, out.at[here], local)
    keep.start()
    for n in range(1, deep):
        slot = spot(lax.rem(z + deep - n, deep), y, core)
        arrived(slot)
        push(out.at[slot], slot, send_y.at[n], to_y)
        push(out.at[slot], slot, send_c.at[n], to_c)
    for n in range(deep):
        slot = spot(lax.rem(z + deep - n, deep), 1 - y, core)
        arrived(slot)
        push(out.at[slot], slot, send_c.at[deep + n], to_c)
    for n in range(deep):
        for yy in (y, 1 - y):
            arrived(spot(lax.rem(z + deep - n, deep), yy, 1 - core))
    keep.wait()
    for copy in sends:
        copy.wait_send()


def gather_line(block, number):
    count = lax.axis_size("sp")
    deep = count // 4
    dma = pltpu.SemaphoreType.DMA
    return pl.pallas_call(
        functools.partial(line_kernel, count),
        out_shape=jax.ShapeDtypeStruct((count,) + block.shape, block.dtype),
        in_specs=[VMEM],
        out_specs=VMEM,
        scratch_shapes=[dma, dma((count,)), dma((max(deep - 1, 1),)), dma((deep,)), dma((2 * deep,))],
        compiler_params=pltpu.CompilerParams(
            collective_id=number, has_side_effects=True, vmem_limit_bytes=ROOM
        ),
    )(block)


def swap_kernel(count, split, *refs):
    kinds = len(split)
    ins, outs = refs[:kinds], refs[kinds : 2 * kinds]
    local, send, recv = refs[2 * kinds :]
    here, me = lax.axis_index("sp"), lax.axis_index("flt")
    peers = [lax.rem(me + step, count) for step in range(1, count)]
    greet([(here, peer) for peer in peers])
    sends, keeps = [], []
    for k in range(kinds):
        for n, peer in enumerate(peers):
            src = ins[k].at[peer] if split[k] else ins[k]
            copy = remote(src, outs[k].at[me], send.at[k, n], recv.at[k, me], (here, peer))
            copy.start()
            sends.append(copy)
        keep = pltpu.make_async_copy(ins[k].at[me] if split[k] else ins[k], outs[k].at[me], local.at[k])
        keep.start()
        keeps.append(keep)
    for k in range(kinds):
        for n, peer in enumerate(peers):
            src = ins[k].at[peer] if split[k] else ins[k]
            remote(src, outs[k].at[peer], send.at[k, n], recv.at[k, peer], (here, peer)).wait_recv()
    for copy in sends:
        copy.wait_send()
    for keep in keeps:
        keep.wait()


def swap(number, *pieces):
    count = lax.axis_size("flt")
    split = tuple(cut for _, cut in pieces)
    arrays = [array for array, _ in pieces]
    dma = pltpu.SemaphoreType.DMA
    shapes = [a.shape if cut else (count,) + a.shape for a, cut in pieces]
    return pl.pallas_call(
        functools.partial(swap_kernel, count, split),
        out_shape=[jax.ShapeDtypeStruct(s, a.dtype) for s, a in zip(shapes, arrays)],
        in_specs=[VMEM] * len(arrays),
        out_specs=[VMEM] * len(arrays),
        scratch_shapes=[
            dma((len(arrays),)),
            dma((len(arrays), max(count - 1, 1))),
            dma((len(arrays), count)),
        ],
        compiler_params=pltpu.CompilerParams(
            collective_id=number, has_side_effects=True, vmem_limit_bytes=ROOM
        ),
    )(*arrays)


def first_kernel(high, wide, x_ref, e_ref, out_ref, moved):
    planes, flat, outs = e_ref.shape
    lane = lax.broadcasted_iota(jnp.int32, (outs, flat), 1)
    row, col = lane // wide, lane % wide
    blank = jnp.zeros((9 * outs, flat), jnp.bfloat16)
    moved[:, 0:flat] = blank
    moved[:, (planes + 1) * flat : (planes + 2) * flat] = blank

    def fill(plane, carry):
        errors = jnp.transpose(e_ref[plane].astype(jnp.float32))
        start = pl.multiple_of((plane + 1) * flat, flat)
        for ky in range(3):
            for kz in range(3):
                by = (ky - 1) * wide + (kz - 1)
                there_y, there_z = row - (ky - 1), col - (kz - 1)
                inside = (there_y >= 0) & (there_y < high) & (there_z >= 0) & (there_z < wide)
                turned_by = pltpu.roll(errors, by % flat, 1) if by else errors
                at = (ky * 3 + kz) * outs
                moved[at : at + outs, pl.ds(start, flat)] = jnp.where(inside, turned_by, 0.0).astype(
                    jnp.bfloat16
                )
        return carry

    lax.fori_loop(0, planes, fill, 0)

    def tap(step, carry):
        kx, ky = step // 3, step % 3
        left = moved[
            pl.ds(pl.multiple_of(ky * 3 * outs, 3 * outs), 3 * outs),
            pl.ds(pl.multiple_of((2 - kx) * flat, flat), planes * flat),
        ]
        out_ref[step] = jnp.dot(left, x_ref[...], preferred_element_type=jnp.float32)
        return carry

    lax.fori_loop(0, 9, tap, 0)


def first_grad(x_cells, errors, high, wide):
    planes, flat, outs = errors.shape
    ins = x_cells.shape[1]
    found = pl.pallas_call(
        functools.partial(first_kernel, high, wide),
        out_shape=jax.ShapeDtypeStruct((9, 3 * outs, ins), jnp.float32),
        in_specs=[VMEM, VMEM],
        out_specs=VMEM,
        scratch_shapes=[pltpu.VMEM((9 * outs, (planes + 2) * flat), jnp.bfloat16)],
        compiler_params=pltpu.CompilerParams(vmem_limit_bytes=ROOM),
        cost_estimate=pl.CostEstimate(
            flops=54 * outs * ins * planes * flat, bytes_accessed=8 * planes * flat * ins, transcendentals=0
        ),
    )(x_cells, errors)
    return jnp.transpose(found.reshape(3, 3, 3, outs, ins), (3, 0, 1, 2, 4))


def second_kernel(high, wide, h_ref, e_ref, out_ref):
    rows, _, flat, ins = h_ref.shape
    cells, outs = e_ref.shape
    errors = jnp.transpose(e_ref[...].astype(jnp.float32))
    lane = lax.broadcasted_iota(jnp.int32, (outs, cells), 1)
    col, line, deep = lane % wide, (lane // wide) % high, lane // flat
    found = {}
    for a in range(2):
        for b in range(2):
            for c in range(2):
                by = a * flat + b * wide + c
                ok = (deep + a < rows) & (line + b < high) & (col + c < wide)
                rolled = pltpu.roll(errors, (cells - by) % cells, 1) if by else errors
                found[a, b, c] = jnp.where(ok, rolled, 0.0).astype(jnp.bfloat16)
    for kx in range(3):
        for ky in range(3):
            for kz in range(3):
                kind = ((kx + 1) % 2 * 2 + (ky + 1) % 2) * 2 + (kz + 1) % 2
                left = found[int(kx == 0), int(ky == 0), int(kz == 0)]
                right = h_ref[:, kind].reshape(cells, ins)
                out_ref[(kx * 3 + ky) * 3 + kz] = jnp.dot(
                    left, right, preferred_element_type=jnp.float32
                )


def second_grad(hidden, errors, high, wide):
    rows, _, flat, ins = hidden.shape
    cells, outs = errors.shape
    found = pl.pallas_call(
        functools.partial(second_kernel, high, wide),
        out_shape=jax.ShapeDtypeStruct((27, outs, ins), jnp.float32),
        in_specs=[VMEM, VMEM],
        out_specs=VMEM,
        compiler_params=pltpu.CompilerParams(vmem_limit_bytes=ROOM),
        cost_estimate=pl.CostEstimate(
            flops=54 * outs * ins * cells, bytes_accessed=32 * cells * ins, transcendentals=0
        ),
    )(hidden, errors)
    return jnp.transpose(found.reshape(3, 3, 3, outs, ins), (3, 0, 1, 2, 4))


def shifted(shard, by):
    peers = lax.axis_size("sp")
    pairs = [(i, i + by) for i in range(peers) if 0 <= i + by < peers]
    return lax.ppermute(shard, "sp", pairs)


def conv_plain(field, kernel, strides, pads, dilate):
    return lax.conv_general_dilated(
        field[None],
        kernel,
        strides,
        pads,
        lhs_dilation=dilate,
        dimension_numbers=("NDHWC", "DHWIO", "NDHWC"),
        preferred_element_type=jnp.float32,
    )[0]


def silu_slope(value):
    sig = jax.nn.sigmoid(value)
    return sig * (1.0 + value * (1.0 - sig))


def forward_taps(kernel):
    return jnp.transpose(kernel, (1, 2, 3, 4, 0))


def turned(kernel):
    return jnp.transpose(kernel[:, ::-1, ::-1, ::-1], (1, 2, 3, 0, 4))


def window(whole, below, above, start, size):
    padded = jnp.pad(whole, ((below, above),) + ((0, 0),) * (whole.ndim - 1))
    return lax.dynamic_slice_in_dim(padded, start, size, 0)


def cut_last(array, count):
    parts = array.reshape(array.shape[:-1] + (count, array.shape[-1] // count))
    return jnp.moveaxis(parts, -2, 0)


def cut_rows(array, count):
    parts = array.reshape((array.shape[0], count, array.shape[1] // count) + array.shape[2:])
    return jnp.moveaxis(parts, 1, 0)


def join_rows(parts):
    moved = jnp.moveaxis(parts, 0, 1)
    return moved.reshape((moved.shape[0], moved.shape[1] * moved.shape[2]) + moved.shape[3:])


def join_last(parts):
    moved = jnp.moveaxis(parts, 0, -2)
    return moved.reshape(moved.shape[:-2] + (moved.shape[-2] * moved.shape[-1],))


def own_term(parts_f32, parts_sent, me):
    mine = lax.broadcasted_iota(jnp.int32, (parts_sent.shape[0],) + (1,) * (parts_sent.ndim - 1), 0) == me
    rest = jnp.sum(jnp.where(mine, 0.0, parts_sent.astype(jnp.float32)), 0)
    return rest + lax.dynamic_index_in_dim(parts_f32, me, 0, keepdims=False)


def per_device(activations, w_first, w_second, cotangent):
    planes = activations.shape[0]
    rows = cotangent.shape[0]
    place, me = lax.axis_index("sp"), lax.axis_index("flt")
    count = lax.axis_size("flt")
    line = lax.axis_size("sp")
    single = (1, 1, 1)
    double = (2, 2, 2)
    x_parts, cot_parts = swap(1, (activations, False), (cut_last(cotangent, count), True))
    x_wide, cot_part = join_rows(x_parts), join_rows(cot_parts)
    high, wide = x_wide.shape[1], x_wide.shape[2]
    ins = x_wide.shape[3]
    x_full = lax.all_gather(x_wide, "sp", axis=0, tiled=True)
    x_near = jnp.concatenate([shifted(x_wide, 1), x_wide, shifted(x_wide[:1], -1)], 0)
    first_pre = conv_plain(x_near, forward_taps(w_first), single, ((0, 0), (1, 1), (1, 1)), single)
    plane = lax.broadcasted_iota(jnp.int32, (planes + 1, 1, 1, 1), 0) + place * planes
    hidden = jnp.where(plane > 0, jax.nn.silu(first_pre), 0.0).astype(jnp.bfloat16)
    (h_parts,) = swap(2, (hidden, False))
    h_wide = join_last(h_parts)
    h_own = h_wide[1:].reshape(rows, 2, high // 2, 2, wide // 2, 2, ins)
    h_own = jnp.transpose(h_own, (0, 1, 3, 5, 2, 4, 6)).reshape(rows, 8, high * wide // 4, ins)
    h_full = lax.all_gather(h_own, "sp", axis=0, tiled=True)
    second_pre = conv_plain(
        h_wide, forward_taps(w_second), double, ((0, 0), (1, 0), (1, 0)), single
    )
    second_err = (cot_part.astype(jnp.float32) * silu_slope(second_pre)).astype(jnp.bfloat16)
    outs = second_err.shape[-1]
    e_full = gather_line(second_err.reshape(-1, outs), 3).reshape((line * rows,) + second_err.shape[1:])
    e_near = window(e_full, 0, 1, place * rows, rows + 1)
    back_hidden = conv_plain(e_near, turned(w_second), single, ((1, 0), (1, 2), (1, 2)), double)
    back_parts = cut_last(back_hidden, count)
    section_parts = cut_rows(jax.nn.silu(second_pre), count)
    got, section_got = swap(4, (back_parts.astype(jnp.bfloat16), True), (section_parts, True))
    section_out = join_last(section_got)
    hidden_err = own_term(back_parts, got, me)
    first_err = (hidden_err * silu_slope(first_pre[1:])).astype(jnp.bfloat16)
    f_full = gather_line(first_err.reshape(planes, high * wide, outs), 5)
    f_full = f_full.reshape(line * planes, high * wide, outs)
    f_near = window(f_full, 1, 1, place * planes, planes + 2).reshape(planes + 2, high, wide, outs)
    back_input = conv_plain(f_near, turned(w_first), single, ((0, 0), (1, 1), (1, 1)), single)
    in_parts = cut_rows(back_input, count)
    (in_got,) = swap(6, (in_parts.astype(jnp.bfloat16), True))
    grad_input = own_term(in_parts, in_got, me)
    grad_second = second_grad(h_full, e_full.reshape(-1, outs), high // 2, wide // 2)
    grad_first = first_grad(x_full.reshape(-1, ins), f_full, high, wide)
    return (section_out, grad_input, grad_first, grad_second)


def solution(mesh):
    placed = (
        P("sp", "flt", None, None),
        P("flt", None, None, None, None),
        P("flt", None, None, None, None),
        P("sp", "flt", None, None),
    )
    return jax.shard_map(
        per_device,
        mesh=mesh,
        in_specs=placed,
        out_specs=(
            P("sp", "flt", None, None),
            P("sp", "flt", None, None),
            P("flt", None, None, None, None),
            P("flt", None, None, None, None),
        ),
        check_vma=False,
    )
```

profile of v0, /device:TPU:0, one launch (start us, length us, event | category | flops | bytes accessed | tf_op | source)
XLA Modules:
  0.0 134.5 jit_solution(13054669814633183963)
XLA Ops:
  7.2 0.0 copy-start
  7.2 0.0 all-gather.3.cloned.1.call-start
  7.2 1.4 %copy_bitcast_fusion.3.refs_1_ = bf16[2,1,4,4,128]{4,3,2,1,0:T(4,128)(2,1)} fusion(bf16[1,4,4,256]{3,2,1,0:T(4,128)(2,1)} %param.7), kind=kLoop, calls=%fused_computation.30 | loop fusion | bytes 16384 | tf_op jit(solution)/shard_map/transpose | solution.py:271
  8.6 6.8 %shard_map.75 = (bf16[2,2,8,8,256]{4,3,2,1,0:T(8,128)(2,1)}, bf16[2,1,4,4,128]{4,3,2,1,0:T(4,128)(2,1)}) custom-call(bf16[2,8,8,256]{3,2,1,0:T(8,128)(2,1)} %refs_0_.1, bf16[2,1,4,4,128]{4,3,2,1,0:T(4,128)(2,1)} %copy_bitcast_fusion.3.refs_1_), custom_call_target="tpu_custom_call" | custom-call | tf_op jit(solution)/shard_map/pallas_call | solution.py:122
  15.5 1.6 %copy.36 = bf16[2,2,8,8,256]{4,3,2,1,0:T(8,128)(2,1)} copy(bf16[2,2,8,8,256]{4,3,2,0,1:T(8,128)(2,1)} %bitcast.81) | data formatting | bytes 262144 | tf_op jit(solution)/shard_map/transpose | solution.py:280
  17.0 0.0 all-gather.3.cloned.1.call-update
  17.0 0.0 all-gather.5.cloned.1.call-start
  17.1 1.3 collective-permute-start
  18.4 0.8 slice.21
  19.2 1.3 collective-permute-start.1
  20.6 4.1 %collective-permute-done.1 = bf16[1,16,8,256]{3,2,1,0:T(8,128)(2,1)S(1)} collective-permute-done((bf16[1,16,8,256]{3,2,1,0:T(8,128)(2,1)S(1)}, bf16[1,16,8,256]{3,2,1,0:T(8,128)(2,1)S(1)}, u32[]{:S(2)}, u32[]{:S(2)}) %collective-permute-start.1) | collective-permute-done | bytes 65568 | tf_op jit(solution)/shard_map/ppermute | solution.py:236
  24.7 0.0 collective-permute-done
  24.7 0.9 maximum_bitcast_fusion
  25.6 0.0 copy-done
  25.6 4.1 %fusion = f32[1,3,16,8,128]{4,0,3,2,1:T(1,128)S(1)} fusion(bf16[128,3,3,3,256]{4,0,3,2,1:T(8,128)(2,1)S(1)} %copy-done, bf16[1,5,16,8,256]{4,3,2,1,0:T(8,128)(2,1)S(1)} %maximum_bitcast_fusion), kind=kOutput, calls=%fused_computation.1 | convolution fusion | flops 596901888 | bytes 2293760 | tf_op jit(solution)/shard_map/conv_general_dilated | solution.py:240
  29.7 0.7 select_convert_fusion.refs_0_
  30.5 6.2 %shard_map.76 = bf16[2,3,16,8,128]{4,3,2,1,0:T(8,128)(2,1)} custom-call(bf16[3,16,8,128]{3,2,1,0:T(8,128)(2,1)} %select_convert_fusion.refs_0_), custom_call_target="tpu_custom_call" | custom-call | tf_op jit(solution)/shard_map/pallas_call | solution.py:122
  36.7 0.0 copy-start.1
  36.7 1.0 slice.23
  37.7 0.1 copy.47
  37.8 0.1 reshape.126
  37.9 0.1 copy.48
  38.0 0.7 reshape.127
  38.7 0.0 all-gather.5.cloned.1.call-update
  38.7 0.5 iota_compare_fusion
  39.2 0.7 slice.22
  39.9 0.0 copy-done.1
  39.9 0.0 copy-start.4
  39.9 2.4 %fusion.2 = f32[1,1,8,4,128]{4,0,3,2,1:T(1,128)S(1)} fusion(bf16[128,3,3,3,256]{4,0,3,2,1:T(8,128)(2,1)} %param.6, bf16[1,3,16,8,256]{4,3,2,1,0:T(8,128)(2,1)S(1)} %copy_bitcast_fusion.1), kind=kOutput, calls=%fused_computation.3 | convolution fusion | flops 49741824 | bytes 1982464 | tf_op jit(solution)/shard_map/conv_general_dilated | solution.py:240
  42.3 0.0 copy-start.2
  42.3 0.6 copy-done.2
  42.9 0.0 copy-done.4
  42.9 0.6 fusion.13.own
  43.5 14.9 %shard_map.77 = bf16[16,32,128]{2,1,0:T(8,128)(2,1)} custom-call(bf16[32,128]{1,0:T(8,128)(2,1)} %fusion.13.own), custom_call_target="tpu_custom_call" | custom-call | tf_op jit(solution)/shard_map/pallas_call | solution.py:77
  58.4 0.9 copy.40
  59.4 0.0 copy-start.3
  59.4 2.6 %fusion.11 = f32[1,2,16,8,256]{4,0,3,2,1:T(1,128)S(1)} fusion(bf16[128,3,3,3,256]{4,0,3,2,1:T(8,128)(2,1)} %param.6, bf16[1,2,8,4,128]{4,2,3,1,0:T(8,128)(2,1)S(1)} %fusion.14), kind=kOutput, calls=%fused_computation.23 | convolution fusion | flops 49741824 | bytes 2048000 | tf_op jit(solution)/shard_map/conv_general_dilated | solution.py:240
  62.0 0.0 copy-done.3
  62.0 0.6 divide_multiply_fusion.refs_1_
  62.6 0.7 fusion.6.refs_0_
  63.3 6.2 %shard_map.78 = (bf16[2,2,16,8,128]{4,3,2,1,0:T(8,128)(2,1)}, f32[2,1,4,4,128]{4,3,2,1,0:T(4,128)}) custom-call(bf16[2,2,16,8,128]{4,3,2,1,0:T(8,128)(2,1)} %fusion.6.refs_0_, f32[2,1,4,4,128]{4,3,2,1,0:T(4,128)} %divide_multiply_fusion.refs_1_), custom_call_target="tpu_custom_call" | custom-call | tf_op jit(solution)/shard_map/pallas_call | solution.py:122
  69.5 1.0 select_reduce_fusion.1
  70.5 1.6 %fusion.9.own = bf16[2,128,128]{2,1,0:T(8,128)(2,1)} fusion(f32[2,16,8,128]{3,2,1,0:T(8,128)S(1)} %select_reduce_fusion.1, f32[2,128,128]{2,1,0:T(8,128)} %bitcast.80, f32[2,16,8,2,128]{4,2,3,1,0:T(8,128)S(1)} %bitcast.76, s32[]{:T(128)S(6)} %select_n.27), kind=kLoop, calls=%fused_computation.21 | loop fusion | flops 327680 | bytes 458756 | tf_op jit(solution)/shard_map/convert_element_type | solution.py:330
  72.1 17.7 %shard_map.79 = bf16[16,2,128,128]{3,2,1,0:T(8,128)(2,1)} custom-call(bf16[2,128,128]{2,1,0:T(8,128)(2,1)} %fusion.9.own), custom_call_target="tpu_custom_call" | custom-call | tf_op jit(solution)/shard_map/pallas_call | solution.py:77
  89.8 0.9 fusion.10
  90.8 2.4 %fusion.4 = f32[1,2,16,8,256]{4,0,3,2,1:T(1,128)S(1)} fusion(bf16[128,3,3,3,256]{4,0,3,2,1:T(8,128)(2,1)S(1)} %copy-done, bf16[1,4,16,8,128]{4,3,2,1,0:T(8,128)(2,1)S(1)} %fusion.10), kind=kOutput, calls=%fused_computation.7 | convolution fusion | flops 397934592 | bytes 2162688 | tf_op jit(solution)/shard_map/conv_general_dilated | solution.py:240
  93.2 0.7 copy.70
  93.9 6.0 %shard_map.80 = bf16[2,2,8,8,256]{4,3,2,1,0:T(8,128)(2,1)} custom-call(bf16[2,2,8,8,256]{4,3,2,1,0:T(8,128)(2,1)} %bitcast.78), custom_call_target="tpu_custom_call" | custom-call | tf_op jit(solution)/shard_map/pallas_call | solution.py:122
  99.9 1.0 select_reduce_fusion
  100.9 1.3 copy_bitcast_fusion.2
  102.2 0.7 bitcast_add_fusion
  102.9 0.0 all-gather.3.cloned.1.call-done
  102.9 20.2 %shard_map.81 = f32[9,384,256]{2,1,0:T(8,128)} custom-call(bf16[4096,256]{1,0:T(8,128)(2,1)} %bitcast.87, bf16[32,128,128]{2,1,0:T(8,128)(2,1)} %bitcast.66), custom_call_target="tpu_custom_call" | custom-call | flops 7247757312 | bytes 8388608 | tf_op jit(solution)/shard_map/pallas_call | solution.py:178
  123.1 0.0 all-gather.5.cloned.1.call-done.h_ref
  123.1 4.6 %shard_map.82 = f32[27,128,256]{2,1,0:T(8,128)} custom-call(bf16[16,8,32,256]{3,2,1,0:T(8,128)(2,1)} %all-gather.5.cloned.1.call-done.h_ref, bf16[512,128]{1,0:T(8,128)(2,1)} %bitcast.75), custom_call_target="tpu_custom_call" | custom-call | flops 905969664 | bytes 4194304 | tf_op jit(solution)/shard_map/pallas_call | solution.py:220
  (5 shorter events, 0.1 us)
Async XLA Ops:
  7.2 18.5 %copy-start = (bf16[128,3,3,3,256]{4,0,3,2,1:T(8,128)(2,1)S(1)}, bf16[128,3,3,3,256]{4,0,3,2,1:T(8,128)(2,1)}, u32[]{:S(2)}) copy-start(bf16[128,3,3,3,256]{4,0,3,2,1:T(8,128)(2,1)} %param.5) | copy-start | bytes 5308420
  7.2 95.7 %all-gather.3.cloned.1.call-start = ((), (), s32[]{:S(2)}) async-start(), calls=%async_computation | async-start | bytes 2228224 | tf_op jit(solution)/shard_map/all_gather | solution.py:307
  17.0 106.0 %all-gather.5.cloned.1.call-start = ((), (), s32[]{:S(2)}) async-start(), calls=%async_computation.1 | async-start | bytes 2228224 | tf_op jit(solution)/shard_map/all_gather | solution.py:316
  17.1 7.6 %collective-permute-start = (bf16[2,16,8,256]{3,2,1,0:T(8,128)(2,1)}, bf16[2,16,8,256]{3,2,1,0:T(8,128)(2,1)S(1)}, u32[]{:S(2)}, u32[]{:S(2)}) collective-permute-start(bf16[2,16,8,256]{3,2,1,0:T(8,128)(2,1)} %bitcast.72), channel_id=1, source_target_pairs={{0,2},{2,4},{4,6},{6,8},{8,10},{10,12},{12,14},{14,16},{16,18},{18... | collective-permute-start | bytes 393224 | tf_op jit(solution)/shard_map/ppermute | solution.py:236
  19.2 5.4 %collective-permute-start.1 = (bf16[1,16,8,256]{3,2,1,0:T(8,128)(2,1)S(1)}, bf16[1,16,8,256]{3,2,1,0:T(8,128)(2,1)S(1)}, u32[]{:S(2)}, u32[]{:S(2)}) collective-permute-start(bf16[1,16,8,256]{3,2,1,0:T(8,128)(2,1)S(1)} %bitcast.83), channel_id=1, source_target_pairs={{2,0},{4,2},{6,4},{8,6},{10,8},{12,10},{14,12},{16,14},{18,16},{20... | collective-permute-start | bytes 196616 | tf_op jit(solution)/shard_map/ppermute | solution.py:236
  36.7 3.2 %copy-start.1 = (bf16[2,3,16,8,128]{4,3,2,1,0:T(8,128)(2,1)S(1)}, bf16[2,3,16,8,128]{4,3,2,1,0:T(8,128)(2,1)}, u32[]{:S(2)}) copy-start(bf16[2,3,16,8,128]{4,3,2,1,0:T(8,128)(2,1)} %shard_map.76) | copy-start | bytes 589828
  39.9 3.0 %copy-start.4 = (bf16[2,1,4,4,128]{4,3,2,1,0:T(4,128)(2,1)S(1)}, bf16[2,1,4,4,128]{4,3,2,1,0:T(4,128)(2,1)}, u32[]{:S(2)}) copy-start(bf16[2,1,4,4,128]{4,3,2,1,0:T(4,128)(2,1)} %get-tuple-element.8) | copy-start | bytes 24580
  42.3 0.6 copy-start.2
  59.4 2.6 %copy-start.3 = (f32[1,1,8,4,128]{4,0,3,2,1:T(1,128)S(1)}, f32[1,1,8,4,128]{4,0,3,2,1:T(1,128)}, u32[]{:S(2)}) copy-start(f32[1,1,8,4,128]{4,0,3,2,1:T(1,128)} %copy-done.2) | copy-start | bytes 49156
Sparse Core Ops, SparseCore 0:
  17.2 43.1 all-gather.2
  62.5 43.8 all-gather.4
where the time goes:
time: 135 us
  Pallas kernels  82.6 us (61%)
  between operations  14.3 us (11%)
  local copies, waits for them, and re-layouts  11.7 us (9%)
  matrix products  11.5 us (9%)
  other arithmetic  7.73 us (6%)
  waiting for transfers between devices  4.15 us (3%)
  starting transfers between devices  2.66 us (2%)
    pallas_call x2, Pallas kernels, gather_line(): pl.pallas_call(functools.partial(line_kernel, count), out_shape=jax.Shape...  32.6 us
    pallas_call x4, Pallas kernels, swap(): pl.pallas_call(functools.partial(swap_kernel, count, split), out_shape=[j...  25.2 us
    pallas_call x1, Pallas kernels, first_grad(): pl.pallas_call(functools.partial(first_kernel, high, wide), out_shape=jax...  20.2 us
    conv_general_dilated x4, matrix products, conv_plain(): lax.conv_general_dilated(field[None], kernel, strides, pads, lhs_dilation...  11.5 us
    pallas_call x1, Pallas kernels, second_grad(): pl.pallas_call(functools.partial(second_kernel, high, wide), out_shape=ja...  4.62 us
    ppermute x2, waiting for transfers between devices, shifted(): return lax.ppermute(shard, 'sp', pairs)  4.11 us
  transfers between devices with their start and end apart: 4, of which 1 were waited for; matrix products, arithmetic and copies ran while one was open for 20% of the time, Pallas kernels for 53%

commit v1 on v0

--- a/solution.py
+++ b/solution.py
@@ -340,6 +340,599 @@
     return (section_out, grad_input, grad_first, grad_second)
 
 
+def slope_of(value):
+    sig = 1.0 / (1.0 + jnp.exp(-value))
+    return sig * (1.0 + value * (1.0 - sig))
+
+
+def silu_of(value):
+    return value / (1.0 + jnp.exp(-value))
+
+
+def dot_rows(left, right):
+    return lax.dot_general(left, right, (((1,), (1,)), ((), ())), preferred_element_type=jnp.float32)
+
+
+def dot_plain(left, right):
+    return jnp.dot(left, right, preferred_element_type=jnp.float32)
+
+
+class Line:
+    def __init__(self, own, out, local, send, recv, deep, here, other):
+        self.own, self.out, self.local, self.send, self.recv = own, out, local, send, recv
+        self.deep, self.here, self.other = deep, here, other
+        self.z, self.y, self.core = here // 4, (here // 2) % 2, here % 2
+        self.to_y = (self.spot(self.z, 1 - self.y, self.core), other)
+        self.to_c = (self.spot(self.z, self.y, 1 - self.core), other)
+        self.sends = []
+
+    def spot(self, zz, yy, cc):
+        return (zz * 2 + yy) * 2 + cc
+
+    def far(self):
+        return [
+            (self.spot(lax.rem(self.z + step, self.deep), self.y, self.core), self.other)
+            for step in range(1, self.deep)
+        ]
+
+    def push(self, src, slot, place):
+        copy = remote(src, self.out.at[slot], self.send.at[len(self.sends)], self.recv.at[slot], place)
+        copy.start()
+        self.sends.append(copy)
+
+    def arrived(self, slot):
+        remote(self.own, self.out.at[slot], self.send.at[0], self.recv.at[slot], self.to_y).wait_recv()
+
+    def first(self):
+        for place in self.far():
+            self.push(self.own, self.here, place)
+        self.push(self.own, self.here, self.to_y)
+        self.push(self.own, self.here, self.to_c)
+        self.keep = pltpu.make_async_copy(self.own, self.out.at[self.here], self.local)
+        self.keep.start()
+
+    def second(self):
+        for n in range(1, self.deep):
+            slot = self.spot(lax.rem(self.z + self.deep - n, self.deep), self.y, self.core)
+            self.arrived(slot)
+            self.push(self.out.at[slot], slot, self.to_y)
+            self.push(self.out.at[slot], slot, self.to_c)
+
+    def third(self):
+        for n in range(self.deep):
+            slot = self.spot(lax.rem(self.z + self.deep - n, self.deep), 1 - self.y, self.core)
+            self.arrived(slot)
+            self.push(self.out.at[slot], slot, self.to_c)
+
+    def last(self):
+        for n in range(self.deep):
+            for yy in (self.y, 1 - self.y):
+                self.arrived(self.spot(lax.rem(self.z + self.deep - n, self.deep), yy, 1 - self.core))
+        self.keep.wait()
+        for copy in self.sends:
+            copy.wait_send()
+
+
+def line_sends(deep):
+    return (deep - 1) + 2 + 2 * (deep - 1) + deep
+
+
+def chain_kernel(dims, *refs):
+    count, high, wide, ins, outs = dims
+    x_hbm, w1_hbm, w2_hbm, cot_hbm = refs[:4]
+    sec_out, gin_out, x_full, h_full, e_full, f_full = refs[4:10]
+    (
+        w1, w2, x_near, cot_near, cot_wide, acc, plain, pre, slope, h_own, h_near, sec, e_own, e_next, back_f, back_b,
+        back_got, f_near, f_turn, acc_in, in_b, in_got, own_sem, send_sem, recv_sem, line_local, line_send, line_recv,
+    ) = refs[10:]
+    flat = high * wide
+    nh, nw = high // 2, wide // 2
+    cells = nh * nw
+    half = flat // 2
+    deep = count // 4
+    here, me = lax.axis_index("sp"), lax.axis_index("flt")
+    mate = 1 - me
+    has_up, has_down = here < count - 1, here > 0
+    part, up, up_o = (here, mate), (here + 1, me), (here + 1, mate)
+    down, down_o = (here - 1, me), (here - 1, mate)
+    my_lanes = pl.ds(pl.multiple_of(me * outs, outs), outs)
+    mate_lanes = pl.ds(pl.multiple_of(mate * outs, outs), outs)
+    my_half = pl.ds(pl.multiple_of(me * half, half), half)
+    mate_half = pl.ds(pl.multiple_of(mate * half, half), half)
+
+    load_w1 = pltpu.make_async_copy(w1_hbm, w1, own_sem.at[0])
+    load_w2 = pltpu.make_async_copy(w2_hbm, w2, own_sem.at[1])
+    load_x = pltpu.make_async_copy(x_hbm, x_near.at[1:3, my_half, :], own_sem.at[2])
+    load_cot = pltpu.make_async_copy(
+        cot_hbm.at[:, :, my_lanes], cot_near.at[pl.ds(me * (nh // 2), nh // 2)], own_sem.at[3]
+    )
+    load_x.start()
+    load_cot.start()
+    load_w1.start()
+    load_w2.start()
+
+    def line(number, own, out):
+        return Line(
+            own, out, line_local.at[number], line_send.at[number], line_recv.at[number], deep, here, me
+        )
+
+    x_line = line(0, x_near.at[1:3], x_full)
+    h_line = line(1, h_near.at[4:12], h_full)
+    e_line = line(2, e_own, e_full)
+    f_line = line(3, f_turn, f_full)
+
+    barrier = pltpu.get_barrier_semaphore()
+
+    def hello(place):
+        pl.semaphore_signal(barrier, inc=1, device_id=place, device_id_type=MESH)
+
+    always = [part, x_line.to_y, x_line.to_c] + x_line.far()
+    for place in always:
+        hello(place)
+
+    @pl.when(has_up)
+    def _():
+        hello(up)
+        hello(up_o)
+
+    @pl.when(has_down)
+    def _():
+        hello(down)
+        hello(down_o)
+
+    pl.semaphore_wait(
+        barrier, len(always) + 2 * has_up.astype(jnp.int32) + 2 * has_down.astype(jnp.int32)
+    )
+
+    started = []
+
+    def send(src, dst, slot, place, cond=None):
+        copy = remote(src, dst, send_sem.at[len(started)], recv_sem.at[slot], place)
+        if cond is None:
+            copy.start()
+        else:
+            pl.when(cond)(copy.start)
+        started.append((copy, cond))
+
+    def wait(src, dst, slot, cond=None):
+        copy = remote(src, dst, send_sem.at[0], recv_sem.at[slot], part)
+        if cond is None:
+            copy.wait_recv()
+        else:
+            pl.when(cond)(copy.wait_recv)
+
+    send(x_hbm, x_near.at[1:3, my_half, :], 0, part)
+    send(x_hbm.at[1], x_near.at[0, my_half, :], 1, up, has_up)
+    send(x_hbm.at[1], x_near.at[0, my_half, :], 2, up_o, has_up)
+    send(x_hbm.at[0], x_near.at[3, my_half, :], 3, down, has_down)
+    send(x_hbm.at[0], x_near.at[3, my_half, :], 4, down_o, has_down)
+    cot_rows = pl.ds(me * (nh // 2), nh // 2)
+    cot_rows_mate = pl.ds(mate * (nh // 2), nh // 2)
+    send(cot_hbm.at[:, :, mate_lanes], cot_near.at[cot_rows], 5, part)
+
+    @pl.when(jnp.logical_not(has_down))
+    def _():
+        x_near[0] = jnp.zeros((flat, ins), jnp.bfloat16)
+        h_near[0:4] = jnp.zeros((4, cells, ins), jnp.bfloat16)
+        f_near[0] = jnp.zeros((flat, outs), jnp.bfloat16)
+
+    @pl.when(jnp.logical_not(has_up))
+    def _():
+        x_near[3] = jnp.zeros((flat, ins), jnp.bfloat16)
+        e_next[...] = jnp.zeros((cells, outs), jnp.bfloat16)
+        f_near[3] = jnp.zeros((flat, outs), jnp.bfloat16)
+
+    load_x.wait()
+    wait(x_hbm, x_near.at[1:3, mate_half, :], 0)
+    x_line.first()
+    wait(x_hbm.at[1], x_near.at[0, my_half, :], 1, has_down)
+    wait(x_hbm.at[1], x_near.at[0, mate_half, :], 2, has_down)
+    wait(x_hbm.at[0], x_near.at[3, my_half, :], 3, has_up)
+    wait(x_hbm.at[0], x_near.at[3, mate_half, :], 4, has_up)
+    load_w1.wait()
+
+    for ky in (1, 0, 2):
+        total = None
+        for kx in range(3):
+            left = x_near[kx : kx + 2].reshape(2 * flat, ins)
+            at = kx * 9 + ky * 3
+            right = w1[at : at + 3].reshape(3 * outs, ins)
+            term = dot_rows(left, right)
+            total = term if total is None else total + term
+        total = total.reshape(2, flat, 3 * outs)
+        if ky == 1:
+            acc[...] = total
+        elif ky == 0:
+            acc[:, wide:, :] += total[:, : flat - wide, :]
+        else:
+            acc[:, : flat - wide, :] += total[:, wide:, :]
+    col = lax.broadcasted_iota(jnp.int32, (2 * flat, outs), 0) % wide
+    whole = acc[...].reshape(2 * flat, 3 * outs)
+    value = whole[:, outs : 2 * outs]
+    value = value + jnp.where(col > 0, pltpu.roll(whole[:, :outs], 1, 0), 0.0)
+    value = value + jnp.where(col < wide - 1, pltpu.roll(whole[:, 2 * outs :], 2 * flat - 1, 0), 0.0)
+    plain[...] = value
+
+    def pick(px, py, pz, qz):
+        return pl.ds(px * flat + py * wide + 2 * qz + pz, nh, 2 * wide)
+
+    for px in (1, 0):
+        for py in range(2):
+            for pz in range(2):
+                kind = (px * 2 + py) * 2 + pz
+                found = jnp.concatenate([plain[pick(px, py, pz, qz), :] for qz in range(nw)], 0)
+                pre[kind] = found
+                h_own[kind] = silu_of(found).astype(jnp.bfloat16)
+    send(h_own.at[4:8], h_near.at[0:4, :, my_lanes], 6, up, has_up)
+    send(h_own.at[4:8], h_near.at[0:4, :, my_lanes], 7, up_o, has_up)
+    send(h_own, h_near.at[4:12, :, my_lanes], 8, part)
+    keep_h = pltpu.make_async_copy(h_own, h_near.at[4:12, :, my_lanes], own_sem.at[4])
+    keep_h.start()
+    load_w2.wait()
+    load_cot.wait()
+    wait(cot_hbm.at[:, :, my_lanes], cot_near.at[cot_rows_mate], 5)
+    cot_wide[...] = cot_near[...].astype(jnp.float32)
+    slope[...] = slope_of(pre[...])
+    keep_h.wait()
+    wait(h_own, h_near.at[4:12, :, mate_lanes], 8)
+    h_line.first()
+    wait(h_own.at[4:8], h_near.at[0:4, :, my_lanes], 6, has_down)
+    wait(h_own.at[4:8], h_near.at[0:4, :, mate_lanes], 7, has_down)
+
+    row = lax.broadcasted_iota(jnp.int32, (cells, outs), 0)
+    qy, qz_of = row % nh, row // nh
+
+    def later_y(v):
+        return jnp.where(qy > 0, pltpu.roll(v, 1, 0), 0.0)
+
+    def later_z(v):
+        return jnp.where(qz_of > 0, pltpu.roll(v, nh, 0), 0.0)
+
+    def earlier_y(v):
+        return jnp.where(qy < nh - 1, pltpu.roll(v, cells - 1, 0), 0.0)
+
+    def earlier_z(v):
+        return jnp.where(qz_of < nw - 1, pltpu.roll(v, cells - nh, 0), 0.0)
+
+    sums = {}
+    for ky in range(3):
+        for kz in range(3):
+            for kx in range(3):
+                kind = kx * 4 + (ky != 1) * 2 + (kz != 1)
+                term = dot_rows(h_near[kind], w2[kx * 9 + ky * 3 + kz])
+                key = (ky == 0, kz == 0)
+                sums[key] = sums[key] + term if key in sums else term
+    second = (
+        sums[False, False]
+        + later_y(sums[True, False] + later_z(sums[True, True]))
+        + later_z(sums[False, True])
+    )
+    cot = jnp.concatenate([cot_wide[:, qz, :] for qz in range(nw)], 0)
+    err = (cot * slope_of(second)).astype(jnp.bfloat16)
+    e_own[...] = err
+    send(e_own, e_next, 9, down, has_down)
+    e_line.first()
+    shown = silu_of(second)
+    for qz in range(nw):
+        sec[:, qz, :] = shown[qz * nh : (qz + 1) * nh]
+    send(sec.at[cot_rows_mate], sec_out.at[:, :, my_lanes], 10, part)
+    keep_sec = pltpu.make_async_copy(sec.at[cot_rows], sec_out.at[:, :, my_lanes], own_sem.at[5])
+    keep_sec.start()
+    x_line.second()
+
+    wait(e_own, e_next, 9, has_up)
+
+    def variants(block):
+        block = block.astype(jnp.float32)
+        moved_y = earlier_y(block)
+        found = {
+            (0, 0): block,
+            (1, 0): moved_y,
+            (0, 1): earlier_z(block),
+            (1, 1): earlier_z(moved_y),
+        }
+        return {key: v.astype(jnp.bfloat16) for key, v in found.items()}
+
+    e_here, e_after = variants(err), variants(e_next[...])
+    for px in range(2):
+        for py in range(2):
+            for pz in range(2):
+                kind = (px * 2 + py) * 2 + pz
+                total = None
+                for kx in (2, 0) if px else (1,):
+                    for ky in (2, 0) if py else (1,):
+                        for kz in (2, 0) if pz else (1,):
+                            source = e_after if kx == 0 else e_here
+                            left = source[int(ky == 0), int(kz == 0)]
+                            term = dot_plain(left, w2[kx * 9 + ky * 3 + kz])
+                            total = term if total is None else total + term
+                for side in range(2):
+                    piece = total[:, side * outs : (side + 1) * outs]
+                    back_f[side, kind] = piece
+                    back_b[side, kind] = piece.astype(jnp.bfloat16)
+    send(back_b.at[mate], back_got, 11, part)
+    e_line.second()
+    x_line.third()
+    wait(back_b.at[me], back_got, 11)
+    for px in range(2):
+        for py in range(2):
+            for pz in range(2):
+                kind = (px * 2 + py) * 2 + pz
+                total = back_f[me, kind] + back_got[kind].astype(jnp.float32)
+                found = (total * slope[kind]).astype(jnp.bfloat16).astype(jnp.float32)
+                for qz in range(nw):
+                    plain[pick(px, py, pz, qz), :] = found[qz * nh : (qz + 1) * nh]
+    first = plain[...]
+    f_near[1:3] = first.astype(jnp.bfloat16).reshape(2, flat, outs)
+    send(f_near.at[1], f_near.at[3], 12, down, has_down)
+    send(f_near.at[2], f_near.at[0], 13, up, has_up)
+    f_turn[...] = jnp.transpose(first).astype(jnp.bfloat16)
+    f_line.first()
+    h_line.second()
+    wait(f_near.at[1], f_near.at[3], 12, has_up)
+    wait(f_near.at[2], f_near.at[0], 13, has_down)
+
+    for kz in range(3):
+        for ky in (1, 0, 2):
+            total = None
+            for kx in range(3):
+                left = f_near[2 - kx : 4 - kx].reshape(2 * flat, outs)
+                term = dot_plain(left, w1[kx * 9 + ky * 3 + kz])
+                total = term if total is None else total + term
+            total = total.reshape(2, flat, ins)
+            if ky == 1:
+                acc_in[kz] = total
+            elif ky == 0:
+                acc_in[kz, :, : flat - wide, :] += total[:, wide:, :]
+            else:
+                acc_in[kz, :, wide:, :] += total[:, : flat - wide, :]
+    col = lax.broadcasted_iota(jnp.int32, (2 * flat, ins), 0) % wide
+    value = acc_in[1].reshape(2 * flat, ins)
+    value = value + jnp.where(
+        col < wide - 1, pltpu.roll(acc_in[0].reshape(2 * flat, ins), 2 * flat - 1, 0), 0.0
+    )
+    value = value + jnp.where(col > 0, pltpu.roll(acc_in[2].reshape(2 * flat, ins), 1, 0), 0.0)
+    value = value.reshape(2, flat, ins)
+    acc_in[1] = value
+    in_b[...] = value.astype(jnp.bfloat16)
+    send(in_b.at[:, mate_half, :], in_got, 14, part)
+    f_line.second()
+    h_line.third()
+    e_line.third()
+    f_line.third()
+    wait(in_b.at[:, my_half, :], in_got, 14)
+    gin_out[...] = acc_in[1, :, my_half, :] + in_got[...].astype(jnp.float32)
+    wait(sec.at[cot_rows], sec_out.at[:, :, mate_lanes], 10)
+    keep_sec.wait()
+    x_line.last()
+    e_line.last()
+    h_line.last()
+    f_line.last()
+    for copy, cond in started:
+        if cond is None:
+            copy.wait_send()
+        else:
+            pl.when(cond)(copy.wait_send)
+
+
+def chain(x, w1, w2, cot):
+    count = lax.axis_size("sp")
+    planes, high, wide, ins = x.shape
+    high = high * 2
+    outs = w1.shape[1]
+    flat = high * wide
+    nh, nw = high // 2, wide // 2
+    cells = nh * nw
+    deep = count // 4
+    dma = pltpu.SemaphoreType.DMA
+    bf, f32 = jnp.bfloat16, jnp.float32
+    anywhere = pl.BlockSpec(memory_space=pl.ANY)
+    shape = jax.ShapeDtypeStruct
+    return pl.pallas_call(
+        functools.partial(chain_kernel, (count, high, wide, ins, outs)),
+        out_shape=[
+            shape(cot.shape, f32),
+            shape((planes, flat // 2, ins), f32),
+            shape((count, planes, flat, ins), bf),
+            shape((count, 8, cells, ins), bf),
+            shape((count, cells, outs), bf),
+            shape((count, outs, planes * flat), bf),
+        ],
+        in_specs=[anywhere] * 4,
+        out_specs=[anywhere, VMEM] + [anywhere] * 4,
+        scratch_shapes=[
+            pltpu.VMEM(w1.shape, bf),
+            pltpu.VMEM(w2.shape, bf),
+            pltpu.VMEM((4, flat, ins), bf),
+            pltpu.VMEM((nh, nw, outs), bf),
+            pltpu.VMEM((nh, nw, outs), f32),
+            pltpu.VMEM((2, flat, 3 * outs), f32),
+            pltpu.VMEM((2 * flat, outs), f32),
+            pltpu.VMEM((8, cells, outs), f32),
+            pltpu.VMEM((8, cells, outs), f32),
+            pltpu.VMEM((8, cells, outs), bf),
+            pltpu.VMEM((12, cells, ins), bf),
+            pltpu.VMEM((nh, nw, outs), f32),
+            pltpu.VMEM((cells, outs), bf),
+            pltpu.VMEM((cells, outs), bf),
+            pltpu.VMEM((2, 8, cells, outs), f32),
+            pltpu.VMEM((2, 8, cells, outs), bf),
+            pltpu.VMEM((8, cells, outs), bf),
+            pltpu.VMEM((4, flat, outs), bf),
+            pltpu.VMEM((outs, 2 * flat), bf),
+            pltpu.VMEM((3, 2, flat, ins), f32),
+            pltpu.VMEM((2, flat, ins), bf),
+            pltpu.VMEM((2, flat // 2, ins), bf),
+            dma((6,)),
+            dma((15,)),
+            dma((15,)),
+            dma((4,)),
+            dma((4, line_sends(deep))),
+            dma((4, count)),
+        ],
+        compiler_params=pltpu.CompilerParams(
+            collective_id=1, has_side_effects=True, vmem_limit_bytes=ROOM
+        ),
+    )(x.reshape(planes, flat // 2, ins), w1, w2, cot)
+
+
+def filter_kernel(dims, *refs):
+    high, wide, outs, ins = dims
+    sec_in, gin_in, x_hbm, h_hbm, e_hbm, f_hbm = refs[:6]
+    sec_out, gin_out, first_out, second_out = refs[6:10]
+    x_v, h_v, e_v, f_v, moved, found1, found2, in_sem, out_sem = refs[10:]
+    count = f_v.shape[0]
+    flat = high * wide
+    nh, nw = high // 2, wide // 2
+    cells = nh * nw
+    loads = [
+        pltpu.make_async_copy(src, dst, in_sem.at[n])
+        for n, (src, dst) in enumerate(((e_hbm, e_v), (h_hbm, h_v), (f_hbm, f_v), (x_hbm, x_v)))
+    ]
+    for load in loads:
+        load.start()
+    outs_going = [
+        pltpu.make_async_copy(sec_in, sec_out, out_sem.at[0]),
+        pltpu.make_async_copy(gin_in, gin_out, out_sem.at[1]),
+    ]
+    for copy in outs_going:
+        copy.start()
+
+    loads[0].wait()
+    total = count * cells
+    errors = jnp.transpose(e_v[...].reshape(total, outs).astype(jnp.float32))
+    lane = lax.broadcasted_iota(jnp.int32, (outs, total), 1)
+    line, col, place = lane % nh, (lane // nh) % nw, lane // cells
+    turned_by = {}
+    for a in range(2):
+        for b in range(2):
+            for c in range(2):
+                by = a * cells + c * nh + b
+                ok = (place + a < count) & (line + b < nh) & (col + c < nw)
+                rolled = pltpu.roll(errors, total - by, 1) if by else errors
+                turned_by[a, b, c] = jnp.where(ok, rolled, 0.0).astype(jnp.bfloat16)
+    loads[1].wait()
+    for kx in range(3):
+        for ky in range(3):
+            for kz in range(3):
+                kind = ((kx + 1) % 2 * 2 + (ky + 1) % 2) * 2 + (kz + 1) % 2
+                left = turned_by[int(kx == 0), int(ky == 0), int(kz == 0)]
+                right = h_v[:, kind].reshape(total, ins)
+                found2[(kx * 3 + ky) * 3 + kz] = dot_plain(left, right)
+    copy = pltpu.make_async_copy(found2, second_out, out_sem.at[2])
+    copy.start()
+    outs_going.append(copy)
+
+    loads[2].wait()
+    lane = lax.broadcasted_iota(jnp.int32, (outs, flat), 1)
+    row, col = lane // wide, lane % wide
+    blank = jnp.zeros((9 * outs, flat), jnp.bfloat16)
+    moved[:, 0:flat] = blank
+    moved[:, (2 * count + 1) * flat : (2 * count + 2) * flat] = blank
+
+    def fill(block, carry):
+        for p in range(2):
+            errors = f_v[block, :, p * flat : (p + 1) * flat].astype(jnp.float32)
+            start = pl.multiple_of((2 * block + p + 1) * flat, flat)
+            for ky in range(3):
+                for kz in range(3):
+                    by = (ky - 1) * wide + (kz - 1)
+                    there_y, there_z = row - (ky - 1), col - (kz - 1)
+                    inside = (there_y >= 0) & (there_y < high) & (there_z >= 0) & (there_z < wide)
+                    rolled = pltpu.roll(errors, by % flat, 1) if by else errors
+                    at = (ky * 3 + kz) * outs
+                    moved[at : at + outs, pl.ds(start, flat)] = jnp.where(inside, rolled, 0.0).astype(
+                        jnp.bfloat16
+                    )
+        return carry
+
+    lax.fori_loop(0, count, fill, 0)
+    loads[3].wait()
+
+    def tap(step, carry):
+        kx, ky = step // 3, step % 3
+        left = moved[
+            pl.ds(pl.multiple_of(ky * 3 * outs, 3 * outs), 3 * outs),
+            pl.ds(pl.multiple_of((2 - kx) * flat, flat), 2 * count * flat),
+        ]
+        found1[step] = dot_plain(left, x_v[...].reshape(2 * count * flat, ins)).reshape(3, outs, ins)
+        pltpu.make_async_copy(found1.at[step], first_out.at[step], out_sem.at[3 + step]).start()
+        return carry
+
+    lax.fori_loop(0, 9, tap, 0)
+    for step in range(9):
+        pltpu.make_async_copy(found1.at[step], first_out.at[step], out_sem.at[3 + step]).wait()
+    for copy in outs_going:
+        copy.wait()
+
+
+def filters(sec, gin, x_full, h_full, e_full, f_full, high, wide):
+    count, _, cells, ins = h_full.shape
+    outs = e_full.shape[-1]
+    flat = high * wide
+    dma = pltpu.SemaphoreType.DMA
+    bf, f32 = jnp.bfloat16, jnp.float32
+    anywhere = pl.BlockSpec(memory_space=pl.ANY)
+    shape = jax.ShapeDtypeStruct
+    sec, gin, first, second = pl.pallas_call(
+        functools.partial(filter_kernel, (high, wide, outs, ins)),
+        out_shape=[
+            shape(sec.shape, f32),
+            shape(gin.shape, f32),
+            shape((9, 3, outs, ins), f32),
+            shape((27, outs, ins), f32),
+        ],
+        in_specs=[anywhere] * 6,
+        out_specs=[anywhere] * 4,
+        scratch_shapes=[
+            pltpu.VMEM(x_full.shape, bf),
+            pltpu.VMEM(h_full.shape, bf),
+            pltpu.VMEM(e_full.shape, bf),
+            pltpu.VMEM(f_full.shape, bf),
+            pltpu.VMEM((9 * outs, (2 * count + 2) * flat), bf),
+            pltpu.VMEM((9, 3, outs, ins), f32),
+            pltpu.VMEM((27, outs, ins), f32),
+            dma((4,)),
+            dma((12,)),
+        ],
+        compiler_params=pltpu.CompilerParams(vmem_limit_bytes=ROOM),
+    )(sec, gin, x_full, h_full, e_full, f_full)
+
+    def home(found):
+        return jnp.transpose(found.reshape(3, 3, 3, outs, ins), (3, 0, 1, 2, 4))
+
+    return sec, gin, home(first), home(second)
+
+
+def taps_first(kernel):
+    moved = jnp.transpose(kernel, (1, 2, 3, 0, 4))
+    return moved.reshape((27,) + moved.shape[3:])
+
+
+def per_device_pair(activations, w_first, w_second, cotangent):
+    planes, part, wide, ins = activations.shape
+    sec, gin, x_full, h_full, e_full, f_full = chain(
+        activations, taps_first(w_first), taps_first(w_second), cotangent[0]
+    )
+    sec, gin, grad_first, grad_second = filters(sec, gin, x_full, h_full, e_full, f_full, part * 2, wide)
+    return sec[None], gin.reshape(activations.shape), grad_first, grad_second
+
+
+def per_device_any(activations, w_first, w_second, cotangent):
+    planes, part, wide, ins = activations.shape
+    outs = w_first.shape[0]
+    pair = (
+        lax.axis_size("flt") == 2
+        and planes == 2
+        and wide == 8
+        and part % 8 == 0
+        and outs % 128 == 0
+        and cotangent.shape[0] == 1
+    )
+    run = per_device_pair if pair else per_device
+    return run(activations, w_first, w_second, cotangent)
+
+
 def solution(mesh):
     placed = (
         P("sp", "flt", None, None),
@@ -348,7 +941,7 @@
         P("sp", "flt", None, None),
     )
     return jax.shard_map(
-        per_device,
+        per_device_any,
         mesh=mesh,
         in_specs=placed,
         out_specs=(

time: 135 us -> 70.7 us (0.52)
  between operations: 14.3 us -> 0.64 us
  Pallas kernels: 82.6 us -> 69.9 us
  local copies, waits for them, and re-layouts: 11.7 us -> 0 us
  matrix products: 11.5 us -> 0 us
  other arithmetic: 7.73 us -> 0 us
  waiting for transfers between devices: 4.15 us -> 0 us
  starting transfers between devices: 2.66 us -> 0 us
    pallas_call x8 -> x2, Pallas kernels: 82.6 us -> 69.9 us  [the longest x1 54 us: chain(): pl.pallas_call(functools.partial(chain_kernel, (count, high, wide, ins, o...]
    conv_general_dilated x4 -> x0, matrix products: 11.5 us -> none  [conv_plain(): lax.conv_general_dilated(field[None], kernel, strides, pads, lhs_dilation...]
    ppermute x2 -> x0, waiting for transfers between devices: 4.11 us -> none  [shifted(): return lax.ppermute(shard, 'sp', pairs)]
    transpose x3 -> x0, local copies, waits for them, and re-layouts: 3.04 us -> none  [the longest x1 1.57 us: join_rows(): moved = jnp.moveaxis(parts, 0, 1)]
    reshape x4 -> x0, local copies, waits for them, and re-layouts: 3.03 us -> none  [the longest x1 1.33 us: join_last(): moved.reshape(moved.shape[:-2] + (moved.shape[-2] * moved.shape[-1],))]
    convert_element_type x3 -> x0, other arithmetic: 2.95 us -> none  [the longest x1 1.61 us: per_device(): first_err = (hidden_err * silu_slope(first_pre[1:])).astype(jnp.bfloat16)]
    slice x4 -> x0, local copies, waits for them, and re-layouts: 2.63 us -> none  [the longest x2 1.12 us: per_device(): h_own = h_wide[1:].reshape(rows, 2, high // 2, 2, wide // 2, 2, ins)]
    ppermute x2 -> x0, starting transfers between devices: 2.58 us -> none  [shifted(): return lax.ppermute(shard, 'sp', pairs)]
  transfers between devices with their start and end apart: 4 -> 0, of which waited for: 1 -> 0; matrix products, arithmetic and copies ran while one was open for 20% -> 0% of each run, Pallas kernels for 53% -> 0%
where the time goes in v1:
time: 70.7 us; the launch traced here: 70.6 us
  Pallas kernels  69.9 us (99%)
    pallas_call x1, Pallas kernels, chain(): pl.pallas_call(functools.partial(chain_kernel, (count, high, wide, ins, o...  54 us
    pallas_call x1, Pallas kernels, filters(): pl.pallas_call(functools.partial(filter_kernel, (high, wide, outs, ins)),...  15.9 us

profile of v1, /device:TPU:0, one launch (start us, length us, event | category | flops | bytes accessed | tf_op | source)
XLA Modules:
  0.0 70.6 jit_solution(9152502194221305093)
XLA Ops:
  0.6 54.0 %shard_map.75 = (f32[4,4,256]{2,1,0:T(4,128)}, f32[2,64,256]{2,1,0:T(8,128)}, bf16[16,2,128,256]{3,2,1,0:T(8,128)(2,1)}, bf16[16,8,32,256]{3,2,1,0:T(8,128)(2,1)...) custom-call(bf16[2,64,256]{2,1,0:T(8,128)(2,1)} %bitcast.18, bf16[27,128,256]{2,1,0:T(8,128)(2,1)} %bitcast.16, ...), custom_call_target="tpu_custom_call" | custom-call | tf_op jit(solution)/shard_map/pallas_call | solution.py:731
  54.6 15.9 %shard_map.76 = (f32[4,4,256]{2,1,0:T(4,128)}, f32[2,64,256]{2,1,0:T(8,128)}, f32[9,3,128,256]{3,2,1,0:T(8,128)}, f32[27,128,256]{2,1,0:T(8,128)}) custom-call(f32[4,4,256]{2,1,0:T(4,128)} %get-tuple-element.14.refs_0_, f32[2,64,256]{2,1,0:T(8,128)} %get-tuple-element.15.refs_1_, bf16[16,2,128,256]{3,2,1,0:T(8,128)(2,1)} %get-tuple-element.16.refs_2_, ...), custom_call_target="tpu_custom_call" | custom-call | tf_op jit(solution)/shard_map/pallas_call | solution.py:877

commit v2 on v1

--- a/solution.py
+++ b/solution.py
@@ -357,64 +357,90 @@
     return jnp.dot(left, right, preferred_element_type=jnp.float32)
 
 
-class Line:
-    def __init__(self, own, out, local, send, recv, deep, here, other):
-        self.own, self.out, self.local, self.send, self.recv = own, out, local, send, recv
-        self.deep, self.here, self.other = deep, here, other
-        self.z, self.y, self.core = here // 4, (here // 2) % 2, here % 2
-        self.to_y = (self.spot(self.z, 1 - self.y, self.core), other)
-        self.to_c = (self.spot(self.z, self.y, 1 - self.core), other)
+class Spread:
+    def __init__(self, own, block, row, local, send, recv, deep, both, mixed=False):
+        here, me = lax.axis_index("sp"), lax.axis_index("flt")
+        self.own, self.block, self.row = own, block, row
+        self.local, self.send, self.recv, self.deep, self.both = local, send, recv, deep, both
+        self.z, self.y, self.core, self.me = here // 4, (here // 2) % 2, here % 2, me
+        self.to_c = (here + 1 - 2 * self.core, me)
         self.sends = []
-
-    def spot(self, zz, yy, cc):
-        return (zz * 2 + yy) * 2 + cc
-
-    def far(self):
-        return [
-            (self.spot(lax.rem(self.z + step, self.deep), self.y, self.core), self.other)
-            for step in range(1, self.deep)
-        ]
-
-    def push(self, src, slot, place):
-        copy = remote(src, self.out.at[slot], self.send.at[len(self.sends)], self.recv.at[slot], place)
+        self.is_mixed = mixed
+        across = self.core if mixed else 0 * self.core
+        self.near = (self.y + (1 - across) * (1 - 2 * self.y), me + across * (1 - 2 * me))
+        self.next = (self.y + across * (1 - 2 * self.y), me + (1 - across) * (1 - 2 * me))
+        self.both_off = (1 - self.y, 1 - me)
+
+    def at(self, spot):
+        y, part = spot
+        return ((self.z * 2 + y) * 2 + self.core, part)
+
+    def push(self, src, dst, slot, place):
+        copy = remote(src, dst, self.send.at[len(self.sends)], self.recv.at[slot], place)
         copy.start()
         self.sends.append(copy)
 
-    def arrived(self, slot):
-        remote(self.own, self.out.at[slot], self.send.at[0], self.recv.at[slot], self.to_y).wait_recv()
+    def took(self, dst, slot):
+        remote(dst, dst, self.send.at[0], self.recv.at[slot], self.to_c).wait_recv()
+
+    def push_row(self, spot, slot, place):
+        view = self.row(spot[0], self.core, spot[1])
+        self.push(view, view, slot, place)
+
+    def took_row(self, spot, slot, core=None):
+        self.took(self.row(spot[0], self.core if core is None else core, spot[1]), slot)
 
     def first(self):
-        for place in self.far():
-            self.push(self.own, self.here, place)
-        self.push(self.own, self.here, self.to_y)
-        self.push(self.own, self.here, self.to_c)
-        self.keep = pltpu.make_async_copy(self.own, self.out.at[self.here], self.local)
+        mine = self.block(self.z, self.y, self.core, self.me)
+        for step in range(1, self.deep):
+            zz = lax.rem(self.z + step, self.deep)
+            self.push(self.own, mine, step - 1, ((zz * 2 + self.y) * 2 + self.core, self.me))
+        self.keep = pltpu.make_async_copy(self.own, mine, self.local)
         self.keep.start()
 
     def second(self):
-        for n in range(1, self.deep):
-            slot = self.spot(lax.rem(self.z + self.deep - n, self.deep), self.y, self.core)
-            self.arrived(slot)
-            self.push(self.out.at[slot], slot, self.to_y)
-            self.push(self.out.at[slot], slot, self.to_c)
+        for step in range(1, self.deep):
+            zz = lax.rem(self.z + self.deep - step, self.deep)
+            self.took(self.block(zz, self.y, self.core, self.me), step - 1)
+        self.keep.wait()
+        slot = self.deep - 1
+        own = (self.y, self.me)
+        self.push_row(own, slot, self.at(self.near))
+        if self.both:
+            self.push_row(own, slot + 1, self.at(self.next))
+        self.push_row(own, slot + 3, self.to_c)
 
     def third(self):
-        for n in range(self.deep):
-            slot = self.spot(lax.rem(self.z + self.deep - n, self.deep), 1 - self.y, self.core)
-            self.arrived(slot)
-            self.push(self.out.at[slot], slot, self.to_c)
+        slot = self.deep - 1
+        self.took_row(self.near, slot)
+        if self.both:
+            self.push_row(self.near, slot + 2, self.at(self.next))
+        self.push_row(self.near, slot + 4, self.to_c)
+
+    def fourth(self):
+        slot = self.deep - 1
+        if self.both:
+            self.took_row(self.next, slot + 1)
+            self.push_row(self.next, slot + 5, self.to_c)
+            self.took_row(self.both_off, slot + 2)
+            self.push_row(self.both_off, slot + 6, self.to_c)
 
     def last(self):
-        for n in range(self.deep):
-            for yy in (self.y, 1 - self.y):
-                self.arrived(self.spot(lax.rem(self.z + self.deep - n, self.deep), yy, 1 - self.core))
-        self.keep.wait()
+        slot = self.deep - 1
+        near, far = (self.next, self.near) if self.is_mixed else (self.near, self.next)
+        spots = [(self.y, self.me), near, far, self.both_off]
+        for n, spot in enumerate(spots if self.both else spots[:2]):
+            self.took_row(spot, slot + 3 + n, 1 - self.core)
         for copy in self.sends:
             copy.wait_send()
 
 
-def line_sends(deep):
-    return (deep - 1) + 2 + 2 * (deep - 1) + deep
+def spread_sends(deep):
+    return (deep - 1) + 8
+
+
+def spread_slots(deep):
+    return (deep - 1) + 7
 
 
 def chain_kernel(dims, *refs):
@@ -451,22 +477,48 @@
     load_w1.start()
     load_w2.start()
 
-    def line(number, own, out):
-        return Line(
-            own, out, line_local.at[number], line_send.at[number], line_recv.at[number], deep, here, me
+    def spread(number, own, block, row, both, mixed=False):
+        return Spread(
+            own, block, row, line_local.at[number], line_send.at[number], line_recv.at[number], deep, both, mixed
         )
 
-    x_line = line(0, x_near.at[1:3], x_full)
-    h_line = line(1, h_near.at[4:12], h_full)
-    e_line = line(2, e_own, e_full)
-    f_line = line(3, f_turn, f_full)
+    def half_of(part):
+        return pl.ds(pl.multiple_of(part * half, half), half)
+
+    def lanes_of(part):
+        return pl.ds(pl.multiple_of(part * outs, outs), outs)
+
+    x_line = spread(
+        0,
+        x_hbm,
+        lambda zz, yy, cc, part: x_full.at[zz, yy, cc, :, half_of(part), :],
+        lambda yy, cc, part: x_full.at[:, yy, cc, :, half_of(part), :],
+        True,
+        True,
+    )
+    h_line = spread(
+        1,
+        h_own,
+        lambda zz, yy, cc, part: h_full.at[zz, yy, cc, :, :, lanes_of(part)],
+        lambda yy, cc, part: h_full.at[:, yy, cc, :, :, lanes_of(part)],
+        True,
+    )
+    e_line = spread(
+        2, e_own, lambda zz, yy, cc, part: e_full.at[zz, yy, cc], lambda yy, cc, part: e_full.at[:, yy, cc], False
+    )
+    f_line = spread(
+        3, f_turn, lambda zz, yy, cc, part: f_full.at[zz, yy, cc], lambda yy, cc, part: f_full.at[:, yy, cc], False
+    )
 
     barrier = pltpu.get_barrier_semaphore()
 
     def hello(place):
         pl.semaphore_signal(barrier, inc=1, device_id=place, device_id_type=MESH)
 
-    always = [part, x_line.to_y, x_line.to_c] + x_line.far()
+    zz, yy, cc = here // 4, (here // 2) % 2, here % 2
+    always = [part, x_line.to_c, ((zz * 2 + 1 - yy) * 2 + cc, me)]
+    for step in range(1, deep):
+        always.append(((lax.rem(zz + step, deep) * 2 + yy) * 2 + cc, me))
     for place in always:
         hello(place)
 
@@ -509,6 +561,7 @@
     cot_rows = pl.ds(me * (nh // 2), nh // 2)
     cot_rows_mate = pl.ds(mate * (nh // 2), nh // 2)
     send(cot_hbm.at[:, :, mate_lanes], cot_near.at[cot_rows], 5, part)
+    x_line.first()
 
     @pl.when(jnp.logical_not(has_down))
     def _():
@@ -524,7 +577,6 @@
 
     load_x.wait()
     wait(x_hbm, x_near.at[1:3, mate_half, :], 0)
-    x_line.first()
     wait(x_hbm.at[1], x_near.at[0, my_half, :], 1, has_down)
     wait(x_hbm.at[1], x_near.at[0, mate_half, :], 2, has_down)
     wait(x_hbm.at[0], x_near.at[3, my_half, :], 3, has_up)
@@ -566,6 +618,7 @@
     send(h_own.at[4:8], h_near.at[0:4, :, my_lanes], 6, up, has_up)
     send(h_own.at[4:8], h_near.at[0:4, :, my_lanes], 7, up_o, has_up)
     send(h_own, h_near.at[4:12, :, my_lanes], 8, part)
+    h_line.first()
     keep_h = pltpu.make_async_copy(h_own, h_near.at[4:12, :, my_lanes], own_sem.at[4])
     keep_h.start()
     load_w2.wait()
@@ -575,9 +628,9 @@
     slope[...] = slope_of(pre[...])
     keep_h.wait()
     wait(h_own, h_near.at[4:12, :, mate_lanes], 8)
-    h_line.first()
     wait(h_own.at[4:8], h_near.at[0:4, :, my_lanes], 6, has_down)
     wait(h_own.at[4:8], h_near.at[0:4, :, mate_lanes], 7, has_down)
+    x_line.second()
 
     row = lax.broadcasted_iota(jnp.int32, (cells, outs), 0)
     qy, qz_of = row % nh, row // nh
@@ -618,7 +671,6 @@
     send(sec.at[cot_rows_mate], sec_out.at[:, :, my_lanes], 10, part)
     keep_sec = pltpu.make_async_copy(sec.at[cot_rows], sec_out.at[:, :, my_lanes], own_sem.at[5])
     keep_sec.start()
-    x_line.second()
 
     wait(e_own, e_next, 9, has_up)
 
@@ -651,8 +703,8 @@
                     back_f[side, kind] = piece
                     back_b[side, kind] = piece.astype(jnp.bfloat16)
     send(back_b.at[mate], back_got, 11, part)
+    h_line.second()
     e_line.second()
-    x_line.third()
     wait(back_b.at[me], back_got, 11)
     for px in range(2):
         for py in range(2):
@@ -668,7 +720,7 @@
     send(f_near.at[2], f_near.at[0], 13, up, has_up)
     f_turn[...] = jnp.transpose(first).astype(jnp.bfloat16)
     f_line.first()
-    h_line.second()
+    x_line.third()
     wait(f_near.at[1], f_near.at[3], 12, has_up)
     wait(f_near.at[2], f_near.at[0], 13, has_down)
 
@@ -696,10 +748,12 @@
     acc_in[1] = value
     in_b[...] = value.astype(jnp.bfloat16)
     send(in_b.at[:, mate_half, :], in_got, 14, part)
+    e_line.third()
+    h_line.third()
     f_line.second()
-    h_line.third()
-    e_line.third()
+    x_line.fourth()
     f_line.third()
+    h_line.fourth()
     wait(in_b.at[:, my_half, :], in_got, 14)
     gin_out[...] = acc_in[1, :, my_half, :] + in_got[...].astype(jnp.float32)
     wait(sec.at[cot_rows], sec_out.at[:, :, mate_lanes], 10)
@@ -733,10 +787,10 @@
         out_shape=[
             shape(cot.shape, f32),
             shape((planes, flat // 2, ins), f32),
-            shape((count, planes, flat, ins), bf),
-            shape((count, 8, cells, ins), bf),
-            shape((count, cells, outs), bf),
-            shape((count, outs, planes * flat), bf),
+            shape((deep, 2, 2, planes, flat, ins), bf),
+            shape((deep, 2, 2, 8, cells, ins), bf),
+            shape((deep, 2, 2, cells, outs), bf),
+            shape((deep, 2, 2, outs, planes * flat), bf),
         ],
         in_specs=[anywhere] * 4,
         out_specs=[anywhere, VMEM] + [anywhere] * 4,
@@ -767,8 +821,8 @@
             dma((15,)),
             dma((15,)),
             dma((4,)),
-            dma((4, line_sends(deep))),
-            dma((4, count)),
+            dma((4, spread_sends(deep))),
+            dma((4, spread_slots(deep))),
         ],
         compiler_params=pltpu.CompilerParams(
             collective_id=1, has_side_effects=True, vmem_limit_bytes=ROOM
@@ -911,9 +965,8 @@
 
 def per_device_pair(activations, w_first, w_second, cotangent):
     planes, part, wide, ins = activations.shape
-    sec, gin, x_full, h_full, e_full, f_full = chain(
-        activations, taps_first(w_first), taps_first(w_second), cotangent[0]
-    )
+    sec, gin, *gathered = chain(activations, taps_first(w_first), taps_first(w_second), cotangent[0])
+    x_full, h_full, e_full, f_full = (a.reshape((-1,) + a.shape[3:]) for a in gathered)
     sec, gin, grad_first, grad_second = filters(sec, gin, x_full, h_full, e_full, f_full, part * 2, wide)
     return sec[None], gin.reshape(activations.shape), grad_first, grad_second
 

time: 70.7 us -> 59.5 us (0.84)
  Pallas kernels: 69.9 us -> 58.5 us
    pallas_call x1, Pallas kernels: 54 us -> 42.6 us  [chain(): pl.pallas_call(functools.partial(chain_kernel, (count, high, wide, ins, o...]
where the time goes in v2:
time: 59.5 us; the launch traced here: 59.2 us
  Pallas kernels  58.5 us (98%)
  between operations  0.64 us (1%)
    pallas_call x1, Pallas kernels, chain(): pl.pallas_call(functools.partial(chain_kernel, (count, high, wide, ins, o...  42.6 us
    pallas_call x1, Pallas kernels, filters(): pl.pallas_call(functools.partial(filter_kernel, (high, wide, outs, ins)),...  15.9 us

profile of v2, /device:TPU:0, one launch (start us, length us, event | category | flops | bytes accessed | tf_op | source)
XLA Modules:
  0.0 59.2 jit_solution(5805763788616666989)
XLA Ops:
  0.6 42.6 %shard_map.75 = (f32[4,4,256]{2,1,0:T(4,128)}, f32[2,64,256]{2,1,0:T(8,128)}, bf16[4,2,2,2,128,256]{5,4,3,2,1,0:T(8,128)(2,1)}, bf16[4,2,2,8,32,256]{5,4,3,2,1,0...) custom-call(bf16[2,64,256]{2,1,0:T(8,128)(2,1)} %bitcast.26, ...), custom_call_target="tpu_custom_call" | custom-call | tf_op jit(solution)/shard_map/pallas_call | solution.py:785
  43.2 15.9 %shard_map.76 = (f32[4,4,256]{2,1,0:T(4,128)}, f32[2,64,256]{2,1,0:T(8,128)}, f32[9,3,128,256]{3,2,1,0:T(8,128)}, f32[27,128,256]{2,1,0:T(8,128)}) custom-call(f32[4,4,256]{2,1,0:T(4,128)} %get-tuple-element.14.refs_0_, f32[2,64,256]{2,1,0:T(8,128)} %get-tuple-element.15.refs_1_, bf16[16,2,128,256]{3,2,1,0:T(8,128)(2,1)} %bitcast.20, ...), custom_call_target="tpu_custom_call" | custom-call | tf_op jit(solution)/shard_map/pallas_call | solution.py:931

commit v3 on v2

--- a/solution.py
+++ b/solution.py
@@ -10,6 +10,7 @@
 MESH = pl.DeviceIdType.MESH
 VMEM = pl.BlockSpec(memory_space=pltpu.VMEM)
 ROOM = 62 * 1024 * 1024
+GRANT = 2 * 1024 * 1024
 
 
 def remote(src, dst, send, recv, place):
@@ -358,14 +359,14 @@
 
 
 class Spread:
-    def __init__(self, own, block, row, local, send, recv, deep, both, mixed=False):
+    def __init__(self, own, block, local, send, recv, deep, both, mixed=False, cores=True):
         here, me = lax.axis_index("sp"), lax.axis_index("flt")
-        self.own, self.block, self.row = own, block, row
+        self.own, self.block = own, block
         self.local, self.send, self.recv, self.deep, self.both = local, send, recv, deep, both
         self.z, self.y, self.core, self.me = here // 4, (here // 2) % 2, here % 2, me
         self.to_c = (here + 1 - 2 * self.core, me)
         self.sends = []
-        self.is_mixed = mixed
+        self.is_mixed, self.cores = mixed, cores
         across = self.core if mixed else 0 * self.core
         self.near = (self.y + (1 - across) * (1 - 2 * self.y), me + across * (1 - 2 * me))
         self.next = (self.y + across * (1 - 2 * self.y), me + (1 - across) * (1 - 2 * me))
@@ -383,74 +384,87 @@
     def took(self, dst, slot):
         remote(dst, dst, self.send.at[0], self.recv.at[slot], self.to_c).wait_recv()
 
-    def push_row(self, spot, slot, place):
-        view = self.row(spot[0], self.core, spot[1])
-        self.push(view, view, slot, place)
-
-    def took_row(self, spot, slot, core=None):
-        self.took(self.row(spot[0], self.core if core is None else core, spot[1]), slot)
+    def view(self, n, spot, core=None):
+        zz = lax.rem(self.z + self.deep - n, self.deep) if n else self.z
+        return self.block(zz, spot[0], self.core if core is None else core, spot[1])
+
+    def slot(self, kind, n):
+        return kind * self.deep + n
+
+    def hand(self, n, spot, kind, place, src=None):
+        view = self.view(n, spot)
+        self.push(view if src is None else src, view, self.slot(kind, n), place)
 
     def first(self):
         mine = self.block(self.z, self.y, self.core, self.me)
         for step in range(1, self.deep):
             zz = lax.rem(self.z + step, self.deep)
-            self.push(self.own, mine, step - 1, ((zz * 2 + self.y) * 2 + self.core, self.me))
+            self.push(self.own, mine, self.slot(0, step), ((zz * 2 + self.y) * 2 + self.core, self.me))
+        self.share(0, self.own)
         self.keep = pltpu.make_async_copy(self.own, mine, self.local)
         self.keep.start()
 
-    def second(self):
-        for step in range(1, self.deep):
-            zz = lax.rem(self.z + self.deep - step, self.deep)
-            self.took(self.block(zz, self.y, self.core, self.me), step - 1)
-        self.keep.wait()
-        slot = self.deep - 1
+    def share(self, n, src=None):
         own = (self.y, self.me)
-        self.push_row(own, slot, self.at(self.near))
+        self.hand(n, own, 1, self.at(self.near), src)
         if self.both:
-            self.push_row(own, slot + 1, self.at(self.next))
-        self.push_row(own, slot + 3, self.to_c)
-
-    def third(self):
-        slot = self.deep - 1
-        self.took_row(self.near, slot)
-        if self.both:
-            self.push_row(self.near, slot + 2, self.at(self.next))
-        self.push_row(self.near, slot + 4, self.to_c)
-
-    def fourth(self):
-        slot = self.deep - 1
-        if self.both:
-            self.took_row(self.next, slot + 1)
-            self.push_row(self.next, slot + 5, self.to_c)
-            self.took_row(self.both_off, slot + 2)
-            self.push_row(self.both_off, slot + 6, self.to_c)
-
-    def last(self):
-        slot = self.deep - 1
+            self.hand(n, own, 2, self.at(self.next), src)
+        if self.cores:
+            self.hand(n, own, 4, self.to_c, src)
+
+    def line(self, *steps):
+        for n in steps:
+            self.took(self.view(n, (self.y, self.me)), self.slot(0, n))
+            self.share(n)
+
+    def side(self, *steps):
+        for n in steps:
+            self.took(self.view(n, self.near), self.slot(1, n))
+            if self.both:
+                self.hand(n, self.near, 3, self.at(self.next))
+            if self.cores:
+                self.hand(n, self.near, 5, self.to_c)
+
+    def rest(self, *steps):
+        for n in steps:
+            self.took(self.view(n, self.next), self.slot(2, n))
+            self.hand(n, self.next, 6, self.to_c)
+            self.took(self.view(n, self.both_off), self.slot(3, n))
+            self.hand(n, self.both_off, 7, self.to_c)
+
+    def ended(self, *steps):
         near, far = (self.next, self.near) if self.is_mixed else (self.near, self.next)
         spots = [(self.y, self.me), near, far, self.both_off]
-        for n, spot in enumerate(spots if self.both else spots[:2]):
-            self.took_row(spot, slot + 3 + n, 1 - self.core)
+        for n in steps:
+            if n == 0:
+                self.keep.wait()
+            if not self.cores:
+                continue
+            for kind, spot in enumerate(spots if self.both else spots[:2]):
+                self.took(self.view(n, spot, 1 - self.core), self.slot(4 + kind, n))
+
+    def sent(self):
         for copy in self.sends:
             copy.wait_send()
 
 
 def spread_sends(deep):
-    return (deep - 1) + 8
+    return (deep - 1) + 7 * deep
 
 
 def spread_slots(deep):
-    return (deep - 1) + 7
+    return 8 * deep
 
 
 def chain_kernel(dims, *refs):
     count, high, wide, ins, outs = dims
     x_hbm, w1_hbm, w2_hbm, cot_hbm = refs[:4]
-    sec_out, gin_out, x_full, h_full, e_full, f_full = refs[4:10]
+    sec_out, gin_out, found1, found2 = refs[4:8]
     (
         w1, w2, x_near, cot_near, cot_wide, acc, plain, pre, slope, h_own, h_near, sec, e_own, e_next, back_f, back_b,
-        back_got, f_near, f_turn, acc_in, in_b, in_got, own_sem, send_sem, recv_sem, line_local, line_send, line_recv,
-    ) = refs[10:]
+        back_got, f_near, f_turn, acc_in, in_b, in_got, x_full, h_full, e_full, f_full, f_pair, moved,
+        own_sem, send_sem, recv_sem, line_local, line_send, line_recv,
+    ) = refs[8:]
     flat = high * wide
     nh, nw = high // 2, wide // 2
     cells = nh * nw
@@ -458,6 +472,8 @@
     deep = count // 4
     here, me = lax.axis_index("sp"), lax.axis_index("flt")
     mate = 1 - me
+    core = here % 2
+    share = outs // 2
     has_up, has_down = here < count - 1, here > 0
     part, up, up_o = (here, mate), (here + 1, me), (here + 1, mate)
     down, down_o = (here - 1, me), (here - 1, mate)
@@ -477,9 +493,9 @@
     load_w1.start()
     load_w2.start()
 
-    def spread(number, own, block, row, both, mixed=False):
+    def spread(number, own, block, both, mixed=False, cores=True):
         return Spread(
-            own, block, row, line_local.at[number], line_send.at[number], line_recv.at[number], deep, both, mixed
+            own, block, line_local.at[number], line_send.at[number], line_recv.at[number], deep, both, mixed, cores
         )
 
     def half_of(part):
@@ -491,24 +507,20 @@
     x_line = spread(
         0,
         x_hbm,
-        lambda zz, yy, cc, part: x_full.at[zz, yy, cc, :, half_of(part), :],
-        lambda yy, cc, part: x_full.at[:, yy, cc, :, half_of(part), :],
-        True,
+        lambda zz, yy, cc, part: x_full.at[pl.ds(((zz * 2 + yy) * 2 + cc) * 2 + 1, 2), half_of(part), :],
         True,
     )
     h_line = spread(
         1,
         h_own,
         lambda zz, yy, cc, part: h_full.at[zz, yy, cc, :, :, lanes_of(part)],
-        lambda yy, cc, part: h_full.at[:, yy, cc, :, :, lanes_of(part)],
         True,
+        True,
     )
     e_line = spread(
-        2, e_own, lambda zz, yy, cc, part: e_full.at[zz, yy, cc], lambda yy, cc, part: e_full.at[:, yy, cc], False
-    )
-    f_line = spread(
-        3, f_turn, lambda zz, yy, cc, part: f_full.at[zz, yy, cc], lambda yy, cc, part: f_full.at[:, yy, cc], False
-    )
+        2, e_own, lambda zz, yy, cc, part: e_full.at[zz, yy, cc], False
+    )
+    f_line = spread(3, f_pair, lambda zz, yy, cc, part: f_full.at[zz, yy], False, False, False)
 
     barrier = pltpu.get_barrier_semaphore()
 
@@ -562,6 +574,9 @@
     cot_rows_mate = pl.ds(mate * (nh // 2), nh // 2)
     send(cot_hbm.at[:, :, mate_lanes], cot_near.at[cot_rows], 5, part)
     x_line.first()
+
+    x_full[0] = jnp.zeros((flat, ins), jnp.bfloat16)
+    x_full[2 * count + 1] = jnp.zeros((flat, ins), jnp.bfloat16)
 
     @pl.when(jnp.logical_not(has_down))
     def _():
@@ -630,7 +645,7 @@
     wait(h_own, h_near.at[4:12, :, mate_lanes], 8)
     wait(h_own.at[4:8], h_near.at[0:4, :, my_lanes], 6, has_down)
     wait(h_own.at[4:8], h_near.at[0:4, :, mate_lanes], 7, has_down)
-    x_line.second()
+    x_line.line(1)
 
     row = lax.broadcasted_iota(jnp.int32, (cells, outs), 0)
     qy, qz_of = row % nh, row // nh
@@ -665,6 +680,8 @@
     e_own[...] = err
     send(e_own, e_next, 9, down, has_down)
     e_line.first()
+    x_line.line(2, 3)
+    x_line.side(0)
     shown = silu_of(second)
     for qz in range(nw):
         sec[:, qz, :] = shown[qz * nh : (qz + 1) * nh]
@@ -703,8 +720,10 @@
                     back_f[side, kind] = piece
                     back_b[side, kind] = piece.astype(jnp.bfloat16)
     send(back_b.at[mate], back_got, 11, part)
-    h_line.second()
-    e_line.second()
+    x_line.side(1, 2, 3)
+    h_line.line(1, 2, 3)
+    h_line.side(0)
+    e_line.line(1, 2, 3)
     wait(back_b.at[me], back_got, 11)
     for px in range(2):
         for py in range(2):
@@ -718,9 +737,11 @@
     f_near[1:3] = first.astype(jnp.bfloat16).reshape(2, flat, outs)
     send(f_near.at[1], f_near.at[3], 12, down, has_down)
     send(f_near.at[2], f_near.at[0], 13, up, has_up)
-    f_turn[...] = jnp.transpose(first).astype(jnp.bfloat16)
+    f_turn[...] = jnp.transpose(first).astype(jnp.bfloat16).reshape(2, share, 2 * flat)
+    send(f_turn.at[1 - core], f_pair.at[core], 15, x_line.to_c)
+    f_pair[core] = f_turn[core]
+    wait(f_turn.at[core], f_pair.at[1 - core], 15)
     f_line.first()
-    x_line.third()
     wait(f_near.at[1], f_near.at[3], 12, has_up)
     wait(f_near.at[2], f_near.at[0], 13, has_down)
 
@@ -748,20 +769,99 @@
     acc_in[1] = value
     in_b[...] = value.astype(jnp.bfloat16)
     send(in_b.at[:, mate_half, :], in_got, 14, part)
-    e_line.third()
-    h_line.third()
-    f_line.second()
-    x_line.fourth()
-    f_line.third()
-    h_line.fourth()
+    f_line.line(1, 2, 3)
+    x_line.rest(0, 1, 2, 3)
+    e_line.side(0, 1, 2, 3)
+    h_line.side(1, 2, 3)
+    lane = lax.broadcasted_iota(jnp.int32, (share, flat), 1)
+    row, col = lane // wide, lane % wide
+
+    def fill(zz):
+        def one(block, carry):
+            for p in range(2):
+                errors = f_full[zz, block // 2, block % 2, :, p * flat : (p + 1) * flat].astype(jnp.float32)
+                start = pl.multiple_of((2 * block + p) * flat, flat)
+                for ky in range(3):
+                    for kz in range(3):
+                        by = (ky - 1) * wide + (kz - 1)
+                        there_y, there_z = row - (ky - 1), col - (kz - 1)
+                        inside = (there_y >= 0) & (there_y < high) & (there_z >= 0) & (there_z < wide)
+                        rolled = pltpu.roll(errors, by % flat, 1) if by else errors
+                        at = (ky * 3 + kz) * share
+                        moved[at : at + share, pl.ds(start, flat)] = jnp.where(inside, rolled, 0.0).astype(
+                            jnp.bfloat16
+                        )
+            return carry
+
+        lax.fori_loop(0, 4, one, 0)
+
+    def gather_taps(zz, fresh):
+        def tap(kx, carry):
+            right = x_full[pl.ds(zz * 8 + kx, 8)].reshape(8 * flat, ins)
+            term = dot_plain(moved[...], right).reshape(9, share, ins)
+            found1[kx, :, core] = term if fresh else found1[kx, :, core] + term
+            return carry
+
+        lax.fori_loop(0, 3, tap, 0)
+
+    def group(n):
+        return lax.rem(here // 4 + deep - n, deep) if n else here // 4
+
+    f_line.side(0)
+    f_line.ended(0)
+    fill(group(0))
+    x_line.ended(0, 1, 2, 3)
+    gather_taps(group(0), True)
     wait(in_b.at[:, my_half, :], in_got, 14)
     gin_out[...] = acc_in[1, :, my_half, :] + in_got[...].astype(jnp.float32)
     wait(sec.at[cot_rows], sec_out.at[:, :, mate_lanes], 10)
     keep_sec.wait()
-    x_line.last()
-    e_line.last()
-    h_line.last()
-    f_line.last()
+    f_line.side(1)
+    fill(group(1))
+    gather_taps(group(1), False)
+    h_line.rest(0, 1, 2, 3)
+    f_line.side(2)
+    fill(group(2))
+    gather_taps(group(2), False)
+    f_line.side(3)
+    fill(group(3))
+    for kx in range(3):
+        right = x_full[pl.ds(group(deep - 1) * 8 + kx, 8)].reshape(8 * flat, ins)
+        term = dot_plain(moved[...], right)
+        found1[kx, :, core] = found1[kx, :, core] + term.reshape(9, share, ins)
+        send(found1.at[kx, :, core], found1.at[kx, :, core], 16 + kx, x_line.to_c)
+    e_line.ended(0, 1, 2, 3)
+    h_line.ended(0, 1, 2, 3)
+    total = count * cells
+    errors = jnp.transpose(e_full[...].reshape(total, outs).astype(jnp.float32))
+    lane = lax.broadcasted_iota(jnp.int32, (outs, total), 1)
+    spot_y, spot_z, spot_x = lane % nh, (lane // nh) % nw, lane // cells
+    turned_by = {}
+    for a in range(2):
+        for b in range(2):
+            for c in range(2):
+                by = a * cells + c * nh + b
+                ok = (spot_x + a < count) & (spot_y + b < nh) & (spot_z + c < nw)
+                rolled = pltpu.roll(errors, total - by, 1) if by else errors
+                turned_by[a, b, c] = jnp.where(ok, rolled, 0.0).astype(jnp.bfloat16)
+    for kind in range(8):
+        px, py, pz = kind // 4, (kind // 2) % 2, kind % 2
+        taps = [
+            (kx, ky, kz)
+            for kx in ((0, 2) if px else (1,))
+            for ky in ((0, 2) if py else (1,))
+            for kz in ((0, 2) if pz else (1,))
+        ]
+        left = jnp.concatenate([turned_by[int(kx == 0), int(ky == 0), int(kz == 0)] for kx, ky, kz in taps], 0)
+        term = dot_plain(left, h_full[:, :, :, kind].reshape(total, ins))
+        for n, (kx, ky, kz) in enumerate(taps):
+            found2[(kx * 3 + ky) * 3 + kz] = term[n * outs : (n + 1) * outs]
+    for kx in range(3):
+        wait(found1.at[kx, :, core], found1.at[kx, :, 1 - core], 16 + kx)
+    x_line.sent()
+    e_line.sent()
+    h_line.sent()
+    f_line.sent()
     for copy, cond in started:
         if cond is None:
             copy.wait_send()
@@ -787,13 +887,11 @@
         out_shape=[
             shape(cot.shape, f32),
             shape((planes, flat // 2, ins), f32),
-            shape((deep, 2, 2, planes, flat, ins), bf),
-            shape((deep, 2, 2, 8, cells, ins), bf),
-            shape((deep, 2, 2, cells, outs), bf),
-            shape((deep, 2, 2, outs, planes * flat), bf),
+            pltpu.VMEM((3, 9, 2, outs // 2, ins), f32),
+            pltpu.VMEM((27, outs, ins), f32),
         ],
         in_specs=[anywhere] * 4,
-        out_specs=[anywhere, VMEM] + [anywhere] * 4,
+        out_specs=[anywhere, VMEM, VMEM, VMEM],
         scratch_shapes=[
             pltpu.VMEM(w1.shape, bf),
             pltpu.VMEM(w2.shape, bf),
@@ -813,149 +911,48 @@
             pltpu.VMEM((2, 8, cells, outs), bf),
             pltpu.VMEM((8, cells, outs), bf),
             pltpu.VMEM((4, flat, outs), bf),
-            pltpu.VMEM((outs, 2 * flat), bf),
+            pltpu.VMEM((2, outs // 2, 2 * flat), bf),
             pltpu.VMEM((3, 2, flat, ins), f32),
             pltpu.VMEM((2, flat, ins), bf),
             pltpu.VMEM((2, flat // 2, ins), bf),
+            pltpu.VMEM((planes * count + 2, flat, ins), bf),
+            pltpu.VMEM((deep, 2, 2, 8, cells, ins), bf),
+            pltpu.VMEM((deep, 2, 2, cells, outs), bf),
+            pltpu.VMEM((deep, 2, 2, outs // 2, planes * flat), bf),
+            pltpu.VMEM((2, outs // 2, planes * flat), bf),
+            pltpu.VMEM((9 * outs // 2, 8 * flat), bf),
             dma((6,)),
-            dma((15,)),
-            dma((15,)),
+            dma((19,)),
+            dma((19,)),
             dma((4,)),
             dma((4, spread_sends(deep))),
             dma((4, spread_slots(deep))),
         ],
         compiler_params=pltpu.CompilerParams(
-            collective_id=1, has_side_effects=True, vmem_limit_bytes=ROOM
+            collective_id=1, has_side_effects=True, vmem_limit_bytes=40 * 1024 * 1024
         ),
-    )(x.reshape(planes, flat // 2, ins), w1, w2, cot)
-
-
-def filter_kernel(dims, *refs):
-    high, wide, outs, ins = dims
-    sec_in, gin_in, x_hbm, h_hbm, e_hbm, f_hbm = refs[:6]
-    sec_out, gin_out, first_out, second_out = refs[6:10]
-    x_v, h_v, e_v, f_v, moved, found1, found2, in_sem, out_sem = refs[10:]
-    count = f_v.shape[0]
-    flat = high * wide
-    nh, nw = high // 2, wide // 2
-    cells = nh * nw
-    loads = [
-        pltpu.make_async_copy(src, dst, in_sem.at[n])
-        for n, (src, dst) in enumerate(((e_hbm, e_v), (h_hbm, h_v), (f_hbm, f_v), (x_hbm, x_v)))
-    ]
-    for load in loads:
-        load.start()
-    outs_going = [
-        pltpu.make_async_copy(sec_in, sec_out, out_sem.at[0]),
-        pltpu.make_async_copy(gin_in, gin_out, out_sem.at[1]),
-    ]
-    for copy in outs_going:
+    )(*(pltpu.with_memory_space_constraint(a, pltpu.HBM) for a in (x.reshape(planes, flat // 2, ins), w1, w2, cot)))
+
+
+def write_kernel(*refs):
+    sources, places, sem = refs[:4], refs[4:8], refs[8]
+    copies = [pltpu.make_async_copy(src, dst, sem.at[n]) for n, (src, dst) in enumerate(zip(sources, places))]
+    for copy in copies:
         copy.start()
-
-    loads[0].wait()
-    total = count * cells
-    errors = jnp.transpose(e_v[...].reshape(total, outs).astype(jnp.float32))
-    lane = lax.broadcasted_iota(jnp.int32, (outs, total), 1)
-    line, col, place = lane % nh, (lane // nh) % nw, lane // cells
-    turned_by = {}
-    for a in range(2):
-        for b in range(2):
-            for c in range(2):
-                by = a * cells + c * nh + b
-                ok = (place + a < count) & (line + b < nh) & (col + c < nw)
-                rolled = pltpu.roll(errors, total - by, 1) if by else errors
-                turned_by[a, b, c] = jnp.where(ok, rolled, 0.0).astype(jnp.bfloat16)
-    loads[1].wait()
-    for kx in range(3):
-        for ky in range(3):
-            for kz in range(3):
-                kind = ((kx + 1) % 2 * 2 + (ky + 1) % 2) * 2 + (kz + 1) % 2
-                left = turned_by[int(kx == 0), int(ky == 0), int(kz == 0)]
-                right = h_v[:, kind].reshape(total, ins)
-                found2[(kx * 3 + ky) * 3 + kz] = dot_plain(left, right)
-    copy = pltpu.make_async_copy(found2, second_out, out_sem.at[2])
-    copy.start()
-    outs_going.append(copy)
-
-    loads[2].wait()
-    lane = lax.broadcasted_iota(jnp.int32, (outs, flat), 1)
-    row, col = lane // wide, lane % wide
-    blank = jnp.zeros((9 * outs, flat), jnp.bfloat16)
-    moved[:, 0:flat] = blank
-    moved[:, (2 * count + 1) * flat : (2 * count + 2) * flat] = blank
-
-    def fill(block, carry):
-        for p in range(2):
-            errors = f_v[block, :, p * flat : (p + 1) * flat].astype(jnp.float32)
-            start = pl.multiple_of((2 * block + p + 1) * flat, flat)
-            for ky in range(3):
-                for kz in range(3):
-                    by = (ky - 1) * wide + (kz - 1)
-                    there_y, there_z = row - (ky - 1), col - (kz - 1)
-                    inside = (there_y >= 0) & (there_y < high) & (there_z >= 0) & (there_z < wide)
-                    rolled = pltpu.roll(errors, by % flat, 1) if by else errors
-                    at = (ky * 3 + kz) * outs
-                    moved[at : at + outs, pl.ds(start, flat)] = jnp.where(inside, rolled, 0.0).astype(
-                        jnp.bfloat16
-                    )
-        return carry
-
-    lax.fori_loop(0, count, fill, 0)
-    loads[3].wait()
-
-    def tap(step, carry):
-        kx, ky = step // 3, step % 3
-        left = moved[
-            pl.ds(pl.multiple_of(ky * 3 * outs, 3 * outs), 3 * outs),
-            pl.ds(pl.multiple_of((2 - kx) * flat, flat), 2 * count * flat),
-        ]
-        found1[step] = dot_plain(left, x_v[...].reshape(2 * count * flat, ins)).reshape(3, outs, ins)
-        pltpu.make_async_copy(found1.at[step], first_out.at[step], out_sem.at[3 + step]).start()
-        return carry
-
-    lax.fori_loop(0, 9, tap, 0)
-    for step in range(9):
-        pltpu.make_async_copy(found1.at[step], first_out.at[step], out_sem.at[3 + step]).wait()
-    for copy in outs_going:
+    for copy in copies:
         copy.wait()
 
 
-def filters(sec, gin, x_full, h_full, e_full, f_full, high, wide):
-    count, _, cells, ins = h_full.shape
-    outs = e_full.shape[-1]
-    flat = high * wide
-    dma = pltpu.SemaphoreType.DMA
-    bf, f32 = jnp.bfloat16, jnp.float32
+def write(*arrays):
     anywhere = pl.BlockSpec(memory_space=pl.ANY)
-    shape = jax.ShapeDtypeStruct
-    sec, gin, first, second = pl.pallas_call(
-        functools.partial(filter_kernel, (high, wide, outs, ins)),
-        out_shape=[
-            shape(sec.shape, f32),
-            shape(gin.shape, f32),
-            shape((9, 3, outs, ins), f32),
-            shape((27, outs, ins), f32),
-        ],
-        in_specs=[anywhere] * 6,
+    return pl.pallas_call(
+        write_kernel,
+        out_shape=[jax.ShapeDtypeStruct(a.shape, a.dtype) for a in arrays],
+        in_specs=[anywhere] * 4,
         out_specs=[anywhere] * 4,
-        scratch_shapes=[
-            pltpu.VMEM(x_full.shape, bf),
-            pltpu.VMEM(h_full.shape, bf),
-            pltpu.VMEM(e_full.shape, bf),
-            pltpu.VMEM(f_full.shape, bf),
-            pltpu.VMEM((9 * outs, (2 * count + 2) * flat), bf),
-            pltpu.VMEM((9, 3, outs, ins), f32),
-            pltpu.VMEM((27, outs, ins), f32),
-            dma((4,)),
-            dma((12,)),
-        ],
-        compiler_params=pltpu.CompilerParams(vmem_limit_bytes=ROOM),
-    )(sec, gin, x_full, h_full, e_full, f_full)
-
-    def home(found):
-        return jnp.transpose(found.reshape(3, 3, 3, outs, ins), (3, 0, 1, 2, 4))
-
-    return sec, gin, home(first), home(second)
+        scratch_shapes=[pltpu.SemaphoreType.DMA((4,))],
+        compiler_params=pltpu.CompilerParams(vmem_limit_bytes=GRANT),
+    )(*arrays)
 
 
 def taps_first(kernel):
@@ -965,9 +962,14 @@
 
 def per_device_pair(activations, w_first, w_second, cotangent):
     planes, part, wide, ins = activations.shape
-    sec, gin, *gathered = chain(activations, taps_first(w_first), taps_first(w_second), cotangent[0])
-    x_full, h_full, e_full, f_full = (a.reshape((-1,) + a.shape[3:]) for a in gathered)
-    sec, gin, grad_first, grad_second = filters(sec, gin, x_full, h_full, e_full, f_full, part * 2, wide)
+    outs = w_first.shape[0]
+
+    def home(found):
+        return jnp.transpose(found.reshape(3, 3, 3, outs, ins), (3, 0, 1, 2, 4))
+
+    found = chain(activations, taps_first(w_first), taps_first(w_second), cotangent[0])
+    sec, gin, grad_first, grad_second = write(*found)
+    grad_first, grad_second = home(grad_first), home(grad_second)
     return sec[None], gin.reshape(activations.shape), grad_first, grad_second
 
 

time: 59.5 us -> 52.5 us (0.88)
  Pallas kernels: 58.5 us -> 51.7 us
    pallas_call x1, Pallas kernels: 15.9 us -> 3.04 us  [write(): pl.pallas_call(write_kernel, out_shape=[jax.ShapeDtypeStruct(a.shape, a.d...]
    pallas_call x1, Pallas kernels: 42.6 us -> 48.6 us  [chain(): pl.pallas_call(functools.partial(chain_kernel, (count, high, wide, ins, o...]
where the time goes in v3:
time: 52.5 us; the launch traced here: 52.3 us
  Pallas kernels  51.7 us (98%)
  between operations  0.64 us (1%)
    pallas_call x1, Pallas kernels, chain(): pl.pallas_call(functools.partial(chain_kernel, (count, high, wide, ins, o...  48.6 us
    pallas_call x1, Pallas kernels, write(): pl.pallas_call(write_kernel, out_shape=[jax.ShapeDtypeStruct(a.shape, a.d...  3.04 us

profile of v3, /device:TPU:0, one launch (start us, length us, event | category | flops | bytes accessed | tf_op | source)
XLA Modules:
  0.0 52.3 jit_solution(17700486387096191189)
XLA Ops:
  0.6 48.6 %shard_map.75 = (f32[4,4,256]{2,1,0:T(4,128)S(1)}, f32[2,64,256]{2,1,0:T(8,128)S(1)}, f32[3,9,2,64,256]{4,3,2,1,0:T(8,128)S(1)}, f32[27,128,256]{2,1,0:T(8,128)S(1)}) custom-call(bf16[2,64,256]{2,1,0:T(8,128)(2,1)} %bitcast.18, bf16[27,128,256]{2,1,0:T(8,128)(2,1)} %bitcast.16, bf16[27,128,256]{2,1,0:T(8,128)(2,1)} %bitcast.17, bf16[4,4,256]{2,1,0:T(4,128)(2,1)} %bitcast.19), custom_call_target="tpu_custom_call" | custom-call | tf_op jit(solution)/shard_map/pallas_call | solution.py:885
  49.3 3.0 %shard_map.76 = (f32[4,4,256]{2,1,0:T(4,128)}, f32[2,64,256]{2,1,0:T(8,128)}, f32[3,9,2,64,256]{4,3,2,1,0:T(8,128)}, f32[27,128,256]{2,1,0:T(8,128)}) custom-call(f32[4,4,256]{2,1,0:T(4,128)S(1)} %get-tuple-element.12.refs_0_, f32[2,64,256]{2,1,0:T(8,128)S(1)} %get-tuple-element.13.refs_1_, f32[3,9,2,64,256]{4,3,2,1,0:T(8,128)S(1)} %get-tuple-element.14.refs_2_, ...), custom_call_target="tpu_custom_call" | custom-call | tf_op jit(solution)/shard_map/pallas_call | solution.py:948

commit v4 on v3

--- a/solution.py
+++ b/solution.py
@@ -509,12 +509,12 @@
         x_hbm,
         lambda zz, yy, cc, part: x_full.at[pl.ds(((zz * 2 + yy) * 2 + cc) * 2 + 1, 2), half_of(part), :],
         True,
+        True,
     )
     h_line = spread(
         1,
         h_own,
         lambda zz, yy, cc, part: h_full.at[zz, yy, cc, :, :, lanes_of(part)],
-        True,
         True,
     )
     e_line = spread(
@@ -599,13 +599,9 @@
     load_w1.wait()
 
     for ky in (1, 0, 2):
-        total = None
-        for kx in range(3):
-            left = x_near[kx : kx + 2].reshape(2 * flat, ins)
-            at = kx * 9 + ky * 3
-            right = w1[at : at + 3].reshape(3 * outs, ins)
-            term = dot_rows(left, right)
-            total = term if total is None else total + term
+        lefts = [x_near[kx : kx + 2].reshape(2 * flat, ins) for kx in range(3)]
+        rights = [w1[kx * 9 + ky * 3 : kx * 9 + ky * 3 + 3].reshape(3 * outs, ins) for kx in range(3)]
+        total = dot_rows(jnp.concatenate(lefts, 1), jnp.concatenate(rights, 1))
         total = total.reshape(2, flat, 3 * outs)
         if ky == 1:
             acc[...] = total
@@ -645,7 +641,7 @@
     wait(h_own, h_near.at[4:12, :, mate_lanes], 8)
     wait(h_own.at[4:8], h_near.at[0:4, :, my_lanes], 6, has_down)
     wait(h_own.at[4:8], h_near.at[0:4, :, mate_lanes], 7, has_down)
-    x_line.line(1)
+    x_line.line(1, 2)
 
     row = lax.broadcasted_iota(jnp.int32, (cells, outs), 0)
     qy, qz_of = row % nh, row // nh
@@ -662,14 +658,16 @@
     def earlier_z(v):
         return jnp.where(qz_of < nw - 1, pltpu.roll(v, cells - nh, 0), 0.0)
 
-    sums = {}
+    groups = {}
     for ky in range(3):
         for kz in range(3):
             for kx in range(3):
                 kind = kx * 4 + (ky != 1) * 2 + (kz != 1)
-                term = dot_rows(h_near[kind], w2[kx * 9 + ky * 3 + kz])
-                key = (ky == 0, kz == 0)
-                sums[key] = sums[key] + term if key in sums else term
+                groups.setdefault((ky == 0, kz == 0), []).append((h_near[kind], w2[kx * 9 + ky * 3 + kz]))
+    sums = {
+        key: dot_rows(jnp.concatenate([p[0] for p in pairs], 1), jnp.concatenate([p[1] for p in pairs], 1))
+        for key, pairs in groups.items()
+    }
     second = (
         sums[False, False]
         + later_y(sums[True, False] + later_z(sums[True, True]))
@@ -680,7 +678,7 @@
     e_own[...] = err
     send(e_own, e_next, 9, down, has_down)
     e_line.first()
-    x_line.line(2, 3)
+    x_line.line(3)
     x_line.side(0)
     shown = silu_of(second)
     for qz in range(nw):
@@ -707,14 +705,14 @@
         for py in range(2):
             for pz in range(2):
                 kind = (px * 2 + py) * 2 + pz
-                total = None
+                lefts, rights = [], []
                 for kx in (2, 0) if px else (1,):
                     for ky in (2, 0) if py else (1,):
                         for kz in (2, 0) if pz else (1,):
                             source = e_after if kx == 0 else e_here
-                            left = source[int(ky == 0), int(kz == 0)]
-                            term = dot_plain(left, w2[kx * 9 + ky * 3 + kz])
-                            total = term if total is None else total + term
+                            lefts.append(source[int(ky == 0), int(kz == 0)])
+                            rights.append(w2[kx * 9 + ky * 3 + kz])
+                total = dot_plain(jnp.concatenate(lefts, 1), jnp.concatenate(rights, 0))
                 for side in range(2):
                     piece = total[:, side * outs : (side + 1) * outs]
                     back_f[side, kind] = piece
@@ -747,11 +745,9 @@
 
     for kz in range(3):
         for ky in (1, 0, 2):
-            total = None
-            for kx in range(3):
-                left = f_near[2 - kx : 4 - kx].reshape(2 * flat, outs)
-                term = dot_plain(left, w1[kx * 9 + ky * 3 + kz])
-                total = term if total is None else total + term
+            lefts = [f_near[2 - kx : 4 - kx].reshape(2 * flat, outs) for kx in range(3)]
+            rights = [w1[kx * 9 + ky * 3 + kz] for kx in range(3)]
+            total = dot_plain(jnp.concatenate(lefts, 1), jnp.concatenate(rights, 0))
             total = total.reshape(2, flat, ins)
             if ky == 1:
                 acc_in[kz] = total

time: 52.5 us -> 50.9 us (0.970)
  Pallas kernels: 51.7 us -> 50.1 us
    pallas_call x1, Pallas kernels: 48.6 us -> 47.1 us  [chain(): pl.pallas_call(functools.partial(chain_kernel, (count, high, wide, ins, o...]
where the time goes in v4:
time: 50.9 us; the launch traced here: 50.8 us
  Pallas kernels  50.1 us (98%)
  between operations  0.64 us (1%)
    pallas_call x1, Pallas kernels, chain(): pl.pallas_call(functools.partial(chain_kernel, (count, high, wide, ins, o...  47.1 us
    pallas_call x1, Pallas kernels, write(): pl.pallas_call(write_kernel, out_shape=[jax.ShapeDtypeStruct(a.shape, a.d...  3.04 us

profile of v4, /device:TPU:0, one launch (start us, length us, event | category | flops | bytes accessed | tf_op | source)
XLA Modules:
  0.0 50.8 jit_solution(10084705175901638519)
XLA Ops:
  0.6 47.1 %shard_map.75 = (f32[4,4,256]{2,1,0:T(4,128)S(1)}, f32[2,64,256]{2,1,0:T(8,128)S(1)}, f32[3,9,2,64,256]{4,3,2,1,0:T(8,128)S(1)}, f32[27,128,256]{2,1,0:T(8,128)S(1)}) custom-call(bf16[2,64,256]{2,1,0:T(8,128)(2,1)} %bitcast.18, bf16[27,128,256]{2,1,0:T(8,128)(2,1)} %bitcast.16, bf16[27,128,256]{2,1,0:T(8,128)(2,1)} %bitcast.17, bf16[4,4,256]{2,1,0:T(4,128)(2,1)} %bitcast.19), custom_call_target="tpu_custom_call" | custom-call | tf_op jit(solution)/shard_map/pallas_call | solution.py:881
  47.7 3.0 %shard_map.76 = (f32[4,4,256]{2,1,0:T(4,128)}, f32[2,64,256]{2,1,0:T(8,128)}, f32[3,9,2,64,256]{4,3,2,1,0:T(8,128)}, f32[27,128,256]{2,1,0:T(8,128)}) custom-call(f32[4,4,256]{2,1,0:T(4,128)S(1)} %get-tuple-element.12.refs_0_, f32[2,64,256]{2,1,0:T(8,128)S(1)} %get-tuple-element.13.refs_1_, f32[3,9,2,64,256]{4,3,2,1,0:T(8,128)S(1)} %get-tuple-element.14.refs_2_, ...), custom_call_target="tpu_custom_call" | custom-call | tf_op jit(solution)/shard_map/pallas_call | solution.py:944

commit v5 on v4

--- a/solution.py
+++ b/solution.py
@@ -366,6 +366,7 @@
         self.z, self.y, self.core, self.me = here // 4, (here // 2) % 2, here % 2, me
         self.to_c = (here + 1 - 2 * self.core, me)
         self.sends = []
+        self.twin = None
         self.is_mixed, self.cores = mixed, cores
         across = self.core if mixed else 0 * self.core
         self.near = (self.y + (1 - across) * (1 - 2 * self.y), me + across * (1 - 2 * me))
@@ -407,7 +408,7 @@
     def share(self, n, src=None):
         own = (self.y, self.me)
         self.hand(n, own, 1, self.at(self.near), src)
-        if self.both:
+        if self.both and (n or self.twin is None):
             self.hand(n, own, 2, self.at(self.next), src)
         if self.cores:
             self.hand(n, own, 4, self.to_c, src)
@@ -427,7 +428,10 @@
 
     def rest(self, *steps):
         for n in steps:
-            self.took(self.view(n, self.next), self.slot(2, n))
+            if n or self.twin is None:
+                self.took(self.view(n, self.next), self.slot(2, n))
+            else:
+                self.twin.wait()
             self.hand(n, self.next, 6, self.to_c)
             self.took(self.view(n, self.both_off), self.slot(3, n))
             self.hand(n, self.both_off, 7, self.to_c)
@@ -522,6 +526,10 @@
     )
     f_line = spread(3, f_pair, lambda zz, yy, cc, part: f_full.at[zz, yy], False, False, False)
 
+    h_line.twin = pltpu.make_async_copy(
+        h_near.at[4:12, :, mate_lanes], h_line.view(0, h_line.next), own_sem.at[6]
+    )
+
     barrier = pltpu.get_barrier_semaphore()
 
     def hello(place):
@@ -626,8 +634,9 @@
                 found = jnp.concatenate([plain[pick(px, py, pz, qz), :] for qz in range(nw)], 0)
                 pre[kind] = found
                 h_own[kind] = silu_of(found).astype(jnp.bfloat16)
-    send(h_own.at[4:8], h_near.at[0:4, :, my_lanes], 6, up, has_up)
-    send(h_own.at[4:8], h_near.at[0:4, :, my_lanes], 7, up_o, has_up)
+        if px == 1:
+            send(h_own.at[4:8], h_near.at[0:4, :, my_lanes], 6, up, has_up)
+            send(h_own.at[4:8], h_near.at[0:4, :, my_lanes], 7, up_o, has_up)
     send(h_own, h_near.at[4:12, :, my_lanes], 8, part)
     h_line.first()
     keep_h = pltpu.make_async_copy(h_own, h_near.at[4:12, :, my_lanes], own_sem.at[4])
@@ -639,6 +648,7 @@
     slope[...] = slope_of(pre[...])
     keep_h.wait()
     wait(h_own, h_near.at[4:12, :, mate_lanes], 8)
+    h_line.twin.start()
     wait(h_own.at[4:8], h_near.at[0:4, :, my_lanes], 6, has_down)
     wait(h_own.at[4:8], h_near.at[0:4, :, mate_lanes], 7, has_down)
     x_line.line(1, 2)
@@ -917,7 +927,7 @@
             pltpu.VMEM((deep, 2, 2, outs // 2, planes * flat), bf),
             pltpu.VMEM((2, outs // 2, planes * flat), bf),
             pltpu.VMEM((9 * outs // 2, 8 * flat), bf),
-            dma((6,)),
+            dma((7,)),
             dma((19,)),
             dma((19,)),
             dma((4,)),

time: 50.9 us -> 50.8 us (level)
  no operation moved by 1% of the time
where the time goes in v5:
time: 50.8 us; the launch traced here: 50.5 us
  Pallas kernels  49.9 us (98%)
  between operations  0.64 us (1%)
    pallas_call x1, Pallas kernels, chain(): pl.pallas_call(functools.partial(chain_kernel, (count, high, wide, ins, o...  46.9 us
    pallas_call x1, Pallas kernels, write(): pl.pallas_call(write_kernel, out_shape=[jax.ShapeDtypeStruct(a.shape, a.d...  3.04 us

profile of v5, /device:TPU:0, one launch (start us, length us, event | category | flops | bytes accessed | tf_op | source)
XLA Modules:
  0.0 50.5 jit_solution(1830876163214156550)
XLA Ops:
  0.6 46.9 %shard_map.75 = (f32[4,4,256]{2,1,0:T(4,128)S(1)}, f32[2,64,256]{2,1,0:T(8,128)S(1)}, f32[3,9,2,64,256]{4,3,2,1,0:T(8,128)S(1)}, f32[27,128,256]{2,1,0:T(8,128)S(1)}) custom-call(bf16[2,64,256]{2,1,0:T(8,128)(2,1)} %bitcast.18, bf16[27,128,256]{2,1,0:T(8,128)(2,1)} %bitcast.16, bf16[27,128,256]{2,1,0:T(8,128)(2,1)} %bitcast.17, bf16[4,4,256]{2,1,0:T(4,128)(2,1)} %bitcast.19), custom_call_target="tpu_custom_call" | custom-call | tf_op jit(solution)/shard_map/pallas_call | solution.py:891
  47.5 3.0 %shard_map.76 = (f32[4,4,256]{2,1,0:T(4,128)}, f32[2,64,256]{2,1,0:T(8,128)}, f32[3,9,2,64,256]{4,3,2,1,0:T(8,128)}, f32[27,128,256]{2,1,0:T(8,128)}) custom-call(f32[4,4,256]{2,1,0:T(4,128)S(1)} %get-tuple-element.12.refs_0_, f32[2,64,256]{2,1,0:T(8,128)S(1)} %get-tuple-element.13.refs_1_, f32[3,9,2,64,256]{4,3,2,1,0:T(8,128)S(1)} %get-tuple-element.14.refs_2_, ...), custom_call_target="tpu_custom_call" | custom-call | tf_op jit(solution)/shard_map/pallas_call | solution.py:954
